TPU v7x, 256 devices: a whole 4x4x8 slice. The times are simulated.
256 devices in a mesh: section: 2 (over core), seq: 32 (over z, x), head: 4 (over y).
Axes of the slice: x: 4, y: 4, z: 8, core: 2. Of those that a mesh axis runs over, the one named last changes fastest.
Arguments:
- hidden: bfloat16 [2, 16384, 4608], P('section', ('seq', 'head')), may hold values from -80 to 80
- q_weight: bfloat16 [2, 4608, 2048], P('section', None, 'head'), may hold values from -0.09375 to 0.09375
- key_value_weight: bfloat16 [4608, 2, 1024], P('seq', None, 'head'), may hold values from -0.09375 to 0.09375
- o_weight: bfloat16 [2, 2048, 4608], P('section', 'head'), may hold values from -1 to 1
- in_gain: float32 [2, 4608], P('section'), may hold values from 1 to 6
- post_gain: float32 [2, 4608], P('section'), may hold values from 0.25 to 1.75
- positions: int32 [16384], replicated, may hold values from 0 to 8191, as said below
- block_table: int32 [32, 32], replicated, may hold values from 0 to 1, as said below
Outputs:
- layer_out: bfloat16 [2, 16384, 4608], P('section', ('seq', 'head'))
Inputs may be any that keep to these rules, and one draw needn't show every extreme that they name: Tokens form consecutive documents; positions start at 0 at each document's first token and rise by 1; one document has exactly 8192 tokens and none has more; there are at most 15 documents. block_table[i][j] is 1 exactly when j <= i and some token of block i and some token of block j lie in one document of the positions drawn with it; blocks are 512 consecutive tokens.
All inputs are finite; a program needn't handle non-finite values.
Results may differ from a plain program's by a relative error of at most 0.0075.
Values may be sent and summed in bfloat16 or wider, within the bound.
A program may use at most 128 MiB of HBM per device.

v0:
```python
import math

import jax
import jax.numpy as jnp
from jax import lax
from jax.sharding import PartitionSpec as P

HEAD_WIDTH = 128


epsilon = 1e-06
softcap_limit = 50.0
query_scale = 144.0 ** (-0.5)


def shifted(value, axis, steps):
    count = lax.axis_size(axis)
    first, last = (max(0, -steps), min(count, count - steps))
    return lax.ppermute(value, axis, [(source, source + steps) for source in range(first, last)])


def normalize(values):
    return values * lax.rsqrt(jnp.mean(values * values, axis=-1, keepdims=True) + epsilon)


def apply_rotation(values, token_positions):
    half_size = values.shape[-1] // 2
    frequency = 10000.0 ** (-(jnp.arange(half_size, dtype=jnp.float32) * 2.0 / values.shape[-1]))
    angles = token_positions.astype(jnp.float32)[:, None] * frequency[None, :]
    cosine = jnp.cos(angles)[:, None, :]
    sine_part = jnp.sin(angles)[:, None, :]
    first_half = values[..., :half_size]
    second_half = values[..., half_size:]
    return jnp.concatenate(
        [
            first_half * cosine - second_half * sine_part,
            second_half * cosine + first_half * sine_part,
        ],
        axis=-1,
    )


def local(hidden, q_weight, key_value_weight, o_weight, in_gain, post_gain, positions, block_table):
    section_index = lax.axis_index("section")
    shard_index = lax.axis_index("seq")
    gathered = lax.all_gather(hidden[0], "head", axis=0, tiled=True)
    local_rows = gathered.shape[0]
    first_row = shard_index * local_rows
    local_positions = lax.dynamic_slice_in_dim(positions, first_row, local_rows)
    normed = (normalize(gathered.astype(jnp.float32)) * in_gain[0]).astype(jnp.bfloat16)
    query_matrix = jnp.dot(normed, q_weight[0], preferred_element_type=jnp.float32)
    head_count = query_matrix.shape[1] // HEAD_WIDTH
    query_matrix = apply_rotation(
        query_matrix.reshape(local_rows, head_count, HEAD_WIDTH), local_positions
    ).astype(jnp.bfloat16)
    value_width = key_value_weight.shape[2]
    projected_rows = jnp.einsum(
        "td,dce->tce",
        normed,
        lax.all_gather(key_value_weight, "seq", axis=0, tiled=True),
        preferred_element_type=jnp.float32,
    )
    key_heads = value_width // HEAD_WIDTH
    rotated_keys = apply_rotation(
        projected_rows[:, 0].reshape(local_rows, key_heads, HEAD_WIDTH), local_positions
    )
    produced = jnp.stack(
        [rotated_keys.reshape(local_rows, value_width), projected_rows[:, 1]], axis=1
    ).astype(jnp.bfloat16)
    received = shifted(produced, "section", 1)
    shared = jnp.where(section_index == 0, produced, received)
    queries_per_group = head_count // key_heads
    grouped_queries = query_matrix.reshape(local_rows, key_heads, queries_per_group, HEAD_WIDTH)
    query_index = first_row + jnp.arange(local_rows, dtype=jnp.int32)
    query_start = query_index - local_positions
    table_row = block_table[shard_index]
    last_block = block_table.shape[1] - 1

    def add_block(running, key_block, key_first):
        numerator, denominator = running
        block_size = key_block.shape[0]
        key_rows = key_block[:, 0].reshape(block_size, key_heads, HEAD_WIDTH)
        value_rows = key_block[:, 1].reshape(block_size, key_heads, HEAD_WIDTH)
        scores = (
            jnp.einsum(
                "qhgd,khd->hgqk", grouped_queries, key_rows, preferred_element_type=jnp.float32
            )
            * query_scale
        )
        capped = softcap_limit * jnp.tanh(scores / softcap_limit)
        key_index = key_first + jnp.arange(block_size, dtype=jnp.int32)
        key_start = key_index - lax.dynamic_slice_in_dim(positions, key_first, block_size)
        key_allowed = table_row[jnp.clip(key_index // local_rows, 0, last_block)] == 1
        visible = (
            (key_index[None, :] <= query_index[:, None])
            & (key_start[None, :] == query_start[:, None])
            & key_allowed[None, :]
        )
        raised = jnp.where(visible, jnp.exp(capped), 0.0)
        numerator = numerator + jnp.einsum(
            "hgqk,khd->hgqd",
            raised.astype(jnp.bfloat16),
            value_rows,
            preferred_element_type=jnp.float32,
        )
        denominator = denominator + jnp.sum(raised, axis=-1)
        return (numerator, denominator)

    def shard_allowed(key_shard):
        inside = (key_shard >= 0) & (key_shard <= shard_index)
        return inside & (table_row[jnp.clip(key_shard, 0, last_block)] == 1)

    initial_state = (
        jnp.zeros((key_heads, queries_per_group, local_rows, HEAD_WIDTH), jnp.float32),
        jnp.zeros((key_heads, queries_per_group, local_rows), jnp.float32),
    )
    running = initial_state
    incoming = lax.all_gather(shared, "seq", axis=0, tiled=True)
    piece_rows = incoming.shape[0]
    block_size = math.gcd(piece_rows, local_rows)

    def visit_block(carried, block_number):
        key_first = block_number * block_size
        allowed = shard_allowed(key_first // local_rows) | shard_allowed(
            (key_first + block_size - 1) // local_rows
        )
        key_block = lax.dynamic_slice_in_dim(incoming, block_number * block_size, block_size, 0)
        carried = lax.cond(
            allowed,
            lambda accumulated: add_block(accumulated, key_block, key_first),
            lambda accumulated: accumulated,
            carried,
        )
        return (carried, None)

    running, _ = lax.scan(
        visit_block, running, jnp.arange(piece_rows // block_size, dtype=jnp.int32)
    )
    numerator, denominator = running
    attended = jnp.transpose(numerator / denominator[..., None], (2, 0, 1, 3))
    attended = attended.reshape(local_rows, head_count * HEAD_WIDTH).astype(jnp.bfloat16)
    out_proj = o_weight[0]
    summed = lax.psum_scatter(
        jnp.dot(attended, out_proj, preferred_element_type=jnp.float32).astype(jnp.bfloat16),
        "head",
        scatter_dimension=0,
        tiled=True,
    ).astype(jnp.float32)
    residual = hidden[0].astype(jnp.float32)
    return (residual + normalize(summed) * post_gain[0]).astype(jnp.bfloat16)[None]


def solution(mesh):
    placed = (
        P("section", ("seq", "head"), None),
        P("section", None, "head"),
        P("seq", None, "head"),
        P("section", "head", None),
        P("section", None),
        P("section", None),
        P(),
        P(),
    )
    return jax.shard_map(
        local,
        mesh=mesh,
        in_specs=placed,
        out_specs=P("section", ("seq", "head"), None),
        check_vma=False,
    )
```

profile of v0, /device:TPU:1, one launch (start us, length us, event | category | flops | bytes accessed | tf_op | source)
XLA Modules:
  0.0 960.4 jit_solution(8636157455058432472)
XLA Ops:
  6.5 0.7 all-gather.9.cloned.1.call-update
  7.3 1.6 copy.18
  9.0 0.8 reduce.25
  9.8 0.8 dynamic-slice_convert_fusion
  11.1 56.9 %all-gather.9.cloned.1.call-done = bf16[1,512,4608]{2,1,0:T(8,128)(2,1)} async-done(((bf16[1,128,4608]{2,1,0:T(8,128)(2,1)}), bf16[1,512,4608]{2,1,0:T(8,128)(2,1)}) %all-gather.9.cloned.1.call-update) | async-done | bytes 4718608 | tf_op jit(solution)/shard_map/all_gather | solution.py:46
  67.9 3.3 fusion.13
  71.3 79.1 %all-gather.5.cloned.1.call-done = bf16[4608,2,256]{2,0,1:T(8,128)(2,1)} async-done(((bf16[144,2,256]{2,0,1:T(8,128)(2,1)}), bf16[4608,2,256]{2,0,1:T(8,128)(2,1)}) %all-gather.5.cloned.1.call-update) | async-done | bytes 4718608 | tf_op jit(solution)/shard_map/all_gather | solution.py:60
  150.4 7.2 fusion.25
  157.9 1.3 collective-permute-start
  159.2 5.8 collective-permute-done
  164.9 0.9 broadcast_select_fusion
  166.1 6.7 copy.30
  172.7 6.5 fusion.23
  180.3 127.9 %all-gather.7.cloned.1.call-done = bf16[16384,2,256]{0,2,1:T(8,128)(2,1)} async-done(((bf16[512,2,256]{0,2,1:T(8,128)(2,1)}), bf16[16384,2,256]{0,2,1:T(8,128)(2,1)}) %all-gather.7.cloned.1.call-update) | async-done | bytes 16777232 | tf_op jit(solution)/shard_map/all_gather | solution.py:118
  308.3 135.0 %while.18 = (s32[]{:T(128)}, f32[2,2,512,128]{3,2,1,0:T(8,128)S(1)}, f32[2,2,512]{2,1,0:T(2,128)S(1)}, s32[32]{0:T(128)S(1)}, s32[]{:T(128)}, /*index=5*/s32[32]...) while((s32[]{:T(128)}, ...), condition=%wide.region_5.6_spmd.clone, body=%wide.region_1.5_spmd.clone.sunk | while | flops 546747456 | bytes 13454614 | solution.py:136
  309.6 0.7 fusion.37
  311.6 27.9 %conditional.3 = ((f32[2,2,512,128]{3,2,1,0:T(8,128)S(1)}, f32[2,2,512]{2,1,0:T(2,128)S(1)})) conditional(s32[]{:T(128)} %convert_element_type.90, (f32[2,2,512,128]{3,2,1,0:T(8,128)S(1)}, f32[2,2,512]{2,1,0:T(2,128)S(1)}) %tuple.115, (s32[]{:T(128)}, s32[]{:T(128)}, s32[16384]{0:T(1024)}, s32[512]{0:T(512)S(1)}, s32[32]{0:T(128)S(1)}, ...), branch_computations={%region_2.2_spmd, %region_3.4_spmd} | conditional | flops 546747392 | bytes 13451807 | solution.py:128
  311.6 0.7 fusion.28
  312.3 4.4 compare_select_fusion.1
  316.7 0.7 fusion.27
  318.0 15.5 %select_compare_fusion = pred[512]{0:T(512)(128)(4,1)S(1)} fusion(pred[512]{0:T(512)(128)(4,1)S(1)} %get-tuple-element.458, pred[512]{0:T(512)(128)(4,1)S(1)} %get-tuple-element.459, pred[512]{0:T(512)(128)(4,1)S(1)} %get-tuple-element.460, pred[512]{0:T(512)(128)(4,1)S(1)} %get-tuple-element.461, pred[512]{0:T(512)(128)(4,1)S(1)} %get-tuple-element.462, ...), kind=kLoop, calls=%fused_computation.44 | loop fusion | flops 13312 | bytes 15460 | tf_op jit(solution)/shard_map/while/body/eval_jaxpr/cond/branch_1_fun/eq | solution.py:93
  333.5 0.8 dynamic-slice_subtract_fusion
  334.6 1.3 constant_dynamic-slice_fusion
  336.0 1.8 fusion.2
  337.7 1.8 fusion.7
  340.9 0.7 fusion.37
  344.2 0.7 fusion.37
  443.8 6.6 convolution_convert_fusion
  450.4 0.7 copy-done.2
  451.2 498.3 %reduce-scatter.2.cloned.1.call-done = bf16[128,4608]{1,0:T(8,128)(2,1)} async-done(((bf16[512,4608]{1,0:T(8,128)(2,1)}), bf16[128,4608]{1,0:T(8,128)(2,1)}) %reduce-scatter.2.cloned.1.call-update) | async-done | bytes 1179664 | tf_op jit(solution)/shard_map/reduce_scatter | solution.py:143
  949.5 1.6 fusion.18
  951.1 2.8 fusion.22
  (172 shorter events, 42.6 us)
Async XLA Ops:
  6.5 166.2 %copy-start = (s32[32,32]{1,0:T(8,128)S(1)}, s32[32,32]{1,0:T(8,128)}, u32[]{:S(2)}) copy-start(s32[32,32]{1,0:T(8,128)} %param.19) | copy-start | bytes 12292
  6.5 61.4 %all-gather.9.cloned.1.call-start = ((), (), s32[]{:S(2)}) async-start(), calls=%async_computation.4 | async-start | bytes 5898240 | tf_op jit(solution)/shard_map/all_gather | solution.py:46
  7.3 143.1 %all-gather.5.cloned.1.call-start = ((), (), s32[]{:S(2)}) async-start(), calls=%async_computation.1 | async-start | bytes 4866048 | tf_op jit(solution)/shard_map/all_gather | solution.py:60
  8.9 299.3 %all-gather.7.cloned.1.call-start = ((), (), s32[]{:S(2)}) async-start(), calls=%async_computation.2 | async-start | bytes 17301504 | tf_op jit(solution)/shard_map/all_gather | solution.py:118
  157.9 7.1 collective-permute-start
  165.8 783.7 %reduce-scatter.2.cloned.1.call-start = ((), (), s32[]{:S(2)}) async-start(), calls=%async_computation.3 | async-start | bytes 5898240 | tf_op jit(solution)/shard_map/reduce_scatter | solution.py:143
  450.4 0.7 copy-start.2
  450.4 500.7 %copy-start.1 = (bf16[1,128,4608]{2,1,0:T(8,128)(2,1)S(1)}, bf16[1,128,4608]{2,1,0:T(8,128)(2,1)}, u32[]{:S(2)}) copy-start(bf16[1,128,4608]{2,1,0:T(8,128)(2,1)} %param.12) | copy-start | bytes 3538948
Sparse Core Ops, SparseCore 0:
  9.1 58.7 all-gather.8
  70.5 79.8 all-gather.4
  165.9 142.2 all-gather.6
  450.6 498.9 reduce-scatter.1
where the time goes:
time: 968 us; the launch traced here: 960 us
  waiting for transfers between devices  769 us (79%)
  loops' own time  66.9 us (7%)
  local copies, waits for them, and re-layouts  53.2 us (5%)
  other arithmetic  33 us (3%)
  matrix products  23.8 us (2%)
  between operations  13.3 us (1%)
    reduce_scatter x1, waiting for transfers between devices, local(): lax.psum_scatter(jnp.dot(attended, out_proj, preferred_element_type=jnp.f...  498 us
    all_gather x1, waiting for transfers between devices, local(): incoming = lax.all_gather(shared, 'seq', axis=0, tiled=True)  128 us
    all_gather x1, waiting for transfers between devices, local(): lax.all_gather(key_value_weight, 'seq', axis=0, tiled=True)  79.1 us
    another operation x1, loops' own time, local(): lax.scan(visit_block, running, jnp.arange(piece_rows // block_size, dtype...  66.2 us
    all_gather x1, waiting for transfers between devices, local(): gathered = lax.all_gather(hidden[0], 'head', axis=0, tiled=True)  56.9 us
    dynamic_slice x32, local copies, waits for them, and re-layouts, shard_allowed(): return inside & (table_row[jnp.clip(key_shard, 0, last_block)] == 1)  21.4 us
  transfers between devices with their start and end apart: 5, of which 5 were waited for; matrix products, arithmetic and copies ran while one was open for 2% of the time, Pallas kernels for 0%

commit v1 on v0

v1 whole, which is shorter than its diff:
```python
import math

import functools

import jax
import jax.numpy as jnp
from jax import lax
from jax.experimental import pallas as pl
from jax.experimental.pallas import tpu as pltpu
from jax.sharding import PartitionSpec as P

HEAD_WIDTH = 128


epsilon = 1e-06
softcap_limit = 50.0
query_scale = 144.0 ** (-0.5)
RAISE = softcap_limit * math.log2(math.e)
LONGEST = 8192


def shifted(value, axis, steps):
    count = lax.axis_size(axis)
    first, last = (max(0, -steps), min(count, count - steps))
    return lax.ppermute(value, axis, [(source, source + steps) for source in range(first, last)])


def normalize(values):
    return values * lax.rsqrt(jnp.mean(values * values, axis=-1, keepdims=True) + epsilon)


def apply_rotation(values, token_positions):
    half_size = values.shape[-1] // 2
    frequency = 10000.0 ** (-(jnp.arange(half_size, dtype=jnp.float32) * 2.0 / values.shape[-1]))
    angles = token_positions.astype(jnp.float32)[:, None] * frequency[None, :]
    cosine = jnp.cos(angles)[:, None, :]
    sine_part = jnp.sin(angles)[:, None, :]
    first_half = values[..., :half_size]
    second_half = values[..., half_size:]
    return jnp.concatenate(
        [
            first_half * cosine - second_half * sine_part,
            second_half * cosine + first_half * sine_part,
        ],
        axis=-1,
    )


def attention_kernel(window, key_heads, meta, q_ref, kv_ref, start_ref, out_ref, total, wide):
    step = pl.program_id(0)
    rows = q_ref.shape[0]
    heads = q_ref.shape[1] // HEAD_WIDTH
    shard = meta[0]
    block = shard - step
    group = heads // key_heads

    @pl.when(step == 0)
    def _():
        total[...] = jnp.zeros_like(total)
        wide[...] = jnp.ones_like(wide)

    @pl.when(block >= meta[1])
    def _():
        listed = meta[2 + jnp.maximum(block, 0)] == 1
        start = jnp.where(listed, start_ref[:, :1], shard * rows + rows)
        keys = block * rows + lax.broadcasted_iota(jnp.int32, (rows, rows), 1)
        queries = shard * rows + lax.broadcasted_iota(jnp.int32, (rows, rows), 0)
        seen = (keys >= start) & (keys <= queries)
        for kv_head in range(key_heads):
            low = (key_heads + kv_head) * HEAD_WIDTH
            wide[kv_head, :, :HEAD_WIDTH] = kv_ref[:, low : low + HEAD_WIDTH]
        for head in range(heads):
            kv_head = head // group
            key = kv_ref[:, kv_head * HEAD_WIDTH : (kv_head + 1) * HEAD_WIDTH]
            scores = lax.dot_general(
                q_ref[:, head * HEAD_WIDTH : (head + 1) * HEAD_WIDTH],
                key,
                (((1,), (1,)), ((), ())),
                preferred_element_type=jnp.float32,
            )
            raised = jnp.where(seen, jnp.exp2(jnp.tanh(scores) * RAISE), 0.0)
            total[head] += jnp.dot(
                raised.astype(jnp.bfloat16), wide[kv_head], preferred_element_type=jnp.float32
            )

    @pl.when(step == window - 1)
    def _():
        for head in range(heads):
            value = total[head]
            out_ref[:, head * HEAD_WIDTH : (head + 1) * HEAD_WIDTH] = (
                value[:, :HEAD_WIDTH] / value[:, HEAD_WIDTH:]
            ).astype(jnp.bfloat16)


def attention(queries, incoming, starts, meta, key_heads):
    rows, columns = queries.shape
    window = LONGEST // rows + 1
    kv_columns = incoming.shape[1]
    return pl.pallas_call(
        functools.partial(attention_kernel, window, key_heads),
        out_shape=jax.ShapeDtypeStruct((rows, columns), jnp.bfloat16),
        grid_spec=pltpu.PrefetchScalarGridSpec(
            num_scalar_prefetch=1,
            grid=(window,),
            in_specs=[
                pl.BlockSpec((rows, columns), lambda j, meta: (0, 0)),
                pl.BlockSpec(
                    (rows, kv_columns), lambda j, meta: (jnp.maximum(meta[0] - j, meta[1]), 0)
                ),
                pl.BlockSpec((rows, HEAD_WIDTH), lambda j, meta: (0, 0)),
            ],
            out_specs=pl.BlockSpec((rows, columns), lambda j, meta: (0, 0)),
            scratch_shapes=[
                pltpu.VMEM((columns // HEAD_WIDTH, rows, 2 * HEAD_WIDTH), jnp.float32),
                pltpu.VMEM((key_heads, rows, 2 * HEAD_WIDTH), jnp.bfloat16),
            ],
        ),
        compiler_params=pltpu.CompilerParams(vmem_limit_bytes=56 * 2**20),
        name="attention",
    )(meta, queries, incoming, starts)


def local(hidden, q_weight, key_value_weight, o_weight, in_gain, post_gain, positions, block_table):
    section_index = lax.axis_index("section")
    shard_index = lax.axis_index("seq")
    gathered = lax.all_gather(hidden[0], "head", axis=0, tiled=True)
    local_rows = gathered.shape[0]
    first_row = shard_index * local_rows
    local_positions = lax.dynamic_slice_in_dim(positions, first_row, local_rows)
    normed = (normalize(gathered.astype(jnp.float32)) * in_gain[0]).astype(jnp.bfloat16)
    query_matrix = jnp.dot(normed, q_weight[0], preferred_element_type=jnp.float32)
    head_count = query_matrix.shape[1] // HEAD_WIDTH
    query_matrix = apply_rotation(
        query_matrix.reshape(local_rows, head_count, HEAD_WIDTH), local_positions
    )
    query_matrix = (query_matrix * (query_scale / softcap_limit)).astype(jnp.bfloat16)
    query_matrix = query_matrix.reshape(local_rows, head_count * HEAD_WIDTH)
    value_width = key_value_weight.shape[2]
    projected_rows = jnp.einsum(
        "td,dce->tce",
        normed,
        lax.all_gather(key_value_weight, "seq", axis=0, tiled=True),
        preferred_element_type=jnp.float32,
    )
    key_heads = value_width // HEAD_WIDTH
    rotated_keys = apply_rotation(
        projected_rows[:, 0].reshape(local_rows, key_heads, HEAD_WIDTH), local_positions
    )
    produced = jnp.stack(
        [rotated_keys.reshape(local_rows, value_width), projected_rows[:, 1]], axis=1
    ).astype(jnp.bfloat16)
    received = shifted(produced, "section", 1)
    shared = jnp.where(section_index == 0, produced, received)
    incoming = lax.all_gather(shared.reshape(local_rows, -1), "seq", axis=0, tiled=True)
    query_index = first_row + jnp.arange(local_rows, dtype=jnp.int32)
    query_start = query_index - local_positions
    meta = jnp.concatenate(
        [jnp.stack([shard_index, query_start[0] // local_rows]), block_table[shard_index]]
    )
    starts = jnp.broadcast_to(query_start[:, None], (local_rows, HEAD_WIDTH))
    attended = attention(query_matrix, incoming, starts, meta, key_heads)
    out_proj = o_weight[0]
    summed = lax.psum_scatter(
        jnp.dot(attended, out_proj, preferred_element_type=jnp.float32).astype(jnp.bfloat16),
        "head",
        scatter_dimension=0,
        tiled=True,
    ).astype(jnp.float32)
    residual = hidden[0].astype(jnp.float32)
    return (residual + normalize(summed) * post_gain[0]).astype(jnp.bfloat16)[None]


def solution(mesh):
    placed = (
        P("section", ("seq", "head"), None),
        P("section", None, "head"),
        P("seq", None, "head"),
        P("section", "head", None),
        P("section", None),
        P("section", None),
        P(),
        P(),
    )
    return jax.shard_map(
        local,
        mesh=mesh,
        in_specs=placed,
        out_specs=P("section", ("seq", "head"), None),
        check_vma=False,
    )
```

time: 968 us -> 399 us (0.41)
  waiting for transfers between devices: 769 us -> 333 us
  loops' own time: 66.9 us -> 0 us
  local copies, waits for them, and re-layouts: 53.2 us -> 12.5 us
  other arithmetic: 33 us -> 11 us
    reduce_scatter x1, waiting for transfers between devices: 498 us -> 72.8 us  [local(): lax.psum_scatter(jnp.dot(attended, out_proj, preferred_element_type=jnp.f...]
    another operation x33 -> x0, loops' own time: 66.9 us -> none  [the longest x1 66.2 us: local(): lax.scan(visit_block, running, jnp.arange(piece_rows // block_size, dtype...]
    dynamic_slice x64 -> x0, local copies, waits for them, and re-layouts: 40.3 us -> none  [the longest x32 21.4 us: shard_allowed(): return inside & (table_row[jnp.clip(key_shard, 0, last_block)] == 1)]
    eq x1 -> x0, other arithmetic: 15.5 us -> none  [add_block(): table_row[jnp.clip(key_index // local_rows, 0, last_block)] == 1]
    all_gather x1, waiting for transfers between devices: 128 us -> 118 us  [local(): lax.all_gather(shared.reshape(local_rows, -1), 'seq', axis=0, tiled=True)]
  transfers between devices with their start and end apart: 5 -> 5, of which waited for: 5 -> 5; matrix products, arithmetic and copies ran while one was open for 2% -> 6% of each run, Pallas kernels for 0% -> 0%
where the time goes in v1:
time: 399 us; the launch traced here: 398 us
  waiting for transfers between devices  333 us (83%)
  matrix products  18.7 us (5%)
  between operations  15.9 us (4%)
  local copies, waits for them, and re-layouts  12.5 us (3%)
  other arithmetic  11 us (3%)
  Pallas kernels  5.67 us (1%)
    all_gather x1, waiting for transfers between devices, local(): lax.all_gather(shared.reshape(local_rows, -1), 'seq', axis=0, tiled=True)  118 us
    all_gather x1, waiting for transfers between devices, local(): lax.all_gather(key_value_weight, 'seq', axis=0, tiled=True)  79.1 us
    reduce_scatter x1, waiting for transfers between devices, local(): lax.psum_scatter(jnp.dot(attended, out_proj, preferred_element_type=jnp.f...  72.8 us
    all_gather x1, waiting for transfers between devices, local(): gathered = lax.all_gather(hidden[0], 'head', axis=0, tiled=True)  56.9 us
  transfers between devices with their start and end apart: 5, of which 5 were waited for; matrix products, arithmetic and copies ran while one was open for 6% of the time, Pallas kernels for 0%

profile of v1, /device:TPU:1, one launch (start us, length us, event | category | flops | bytes accessed | tf_op | source)
XLA Modules:
  0.0 398.0 jit_solution(18236991132179085904)
XLA Ops:
  6.5 0.7 all-gather.9.cloned.1.call-update
  7.3 1.6 copy.11
  8.9 0.0 all-gather.7.cloned.1.call-start
  9.0 0.8 reduce
  9.8 0.8 dynamic-slice_convert_fusion
  10.5 0.5 multiply_cosine_fusion
  11.1 56.9 %all-gather.9.cloned.1.call-done = bf16[1,512,4608]{2,1,0:T(8,128)(2,1)} async-done(((bf16[1,128,4608]{2,1,0:T(8,128)(2,1)}), bf16[1,512,4608]{2,1,0:T(8,128)(2,1)}) %all-gather.9.cloned.1.call-update) | async-done | bytes 4718608 | tf_op jit(solution)/shard_map/all_gather | solution.py:126
  67.9 3.3 fusion
  71.3 79.1 %all-gather.5.cloned.1.call-done = bf16[4608,2,256]{2,0,1:T(8,128)(2,1)} async-done(((bf16[144,2,256]{2,0,1:T(8,128)(2,1)}), bf16[4608,2,256]{2,0,1:T(8,128)(2,1)}) %all-gather.5.cloned.1.call-update) | async-done | bytes 4718608 | tf_op jit(solution)/shard_map/all_gather | solution.py:142
  150.4 7.2 %fusion.11 = f32[512,2,256]{0,2,1:T(8,128)S(1)} fusion(bf16[4608,2,256]{2,0,1:T(8,128)(2,1)} %all-gather.5.cloned.1.call-done, bf16[1,512,4608]{2,1,0:T(8,128)(2,1)} %all-gather.9.cloned.1.call-done, f32[4608]{0:T(1024)S(1)} %reduce, f32[512]{0:T(512)S(1)} %add_rsqrt_fusion), kind=kOutput, calls=%fused_computation.25 | convolution fusion | flops 2425356288 | bytes 10506240 | tf_op jit(solution)/shard_map/td,dce->tce/dot_general | solution.py:139
  157.7 0.1 subtract_convert_fusion
  157.8 0.1 pad_maximum_fusion
  157.9 1.3 collective-permute-start
  159.2 5.8 %collective-permute-done = bf16[512,2,256]{0,2,1:T(8,128)(2,1)S(1)} collective-permute-done((bf16[512,2,256]{0,2,1:T(8,128)(2,1)S(1)}, bf16[512,2,256]{0,2,1:T(8,128)(2,1)S(1)}, u32[]{:S(2)}, u32[]{:S(2)}) %collective-permute-start) | collective-permute-done | bytes 524320 | tf_op jit(solution)/shard_map/ppermute | solution.py:25
  164.9 0.1 broadcast_select_fusion
  165.0 1.0 copy.15
  166.0 0.0 reduce-scatter.2.cloned.1.call-start
  166.1 0.5 slice.22
  169.2 6.8 %copy.13 = bf16[512,4608]{1,0:T(8,128)(2,1)} copy(bf16[512,4608]{0,1:T(8,128)(2,1)} %bitcast.34) | data formatting | bytes 9437184 | tf_op jit(solution)/shard_map/dot_general | solution.py:131
  176.0 0.6 pad_add_fusion.meta
  176.6 6.2 %fusion.13 = f32[512,4,128]{0,2,1:T(8,128)S(1)} fusion(bf16[4,128,4608]{2,1,0:T(8,128)(2,1)} %bitcast.35, bf16[1,512,4608]{2,1,0:T(8,128)(2,1)} %all-gather.9.cloned.1.call-done, f32[4608]{0:T(1024)S(1)} %reduce, f32[512]{0:T(512)S(1)} %add_rsqrt_fusion), kind=kOutput, calls=%fused_computation.26 | convolution fusion | flops 2425356288 | bytes 10506240 | tf_op jit(solution)/shard_map/dot_general | solution.py:131
  182.9 0.2 multiply_subtract_fusion
  183.0 0.1 fusion.10
  183.2 1.0 copy.14.q_ref
  184.2 117.6 %all-gather.7.cloned.1.call-done.kv_ref = bf16[16384,512]{1,0:T(8,128)(2,1)} async-done(((bf16[512,512]{1,0:T(8,128)(2,1)}), bf16[16384,512]{1,0:T(8,128)(2,1)}) %all-gather.7.cloned.1.call-update) | async-done | bytes 16777232 | tf_op jit(solution)/shard_map/all_gather | solution.py:154
  301.8 0.8 broadcast_in_dim.4.start_ref
  302.6 5.7 %attention.1 = bf16[512,512]{1,0:T(8,128)(2,1)} custom-call(s32[34]{0:T(128)} %pad_add_fusion.meta, bf16[512,512]{1,0:T(8,128)(2,1)} %copy.14.q_ref, bf16[16384,512]{1,0:T(8,128)(2,1)} %all-gather.7.cloned.1.call-done.kv_ref, s32[512,128]{1,0:T(8,128)} %broadcast_in_dim.4.start_ref), custom_call_target="tpu_custom_call" | custom-call | tf_op jit(solution)/shard_map/attention/pallas_call | solution.py:99
  308.3 5.3 %convolution_convert_fusion = bf16[512,4608]{1,0:T(8,128)(2,1)} fusion(bf16[512,512]{1,0:T(8,128)(2,1)} %attention.1, bf16[1,512,4608]{2,1,0:T(8,128)(2,1)S(1)} %bitcast.42), kind=kOutput, calls=%fused_computation.5 | convolution fusion | flops 2418278400 | bytes 9961472 | tf_op jit(solution)/shard_map/dot_general | solution.py:164
  313.6 0.7 copy-done.2
  314.4 72.8 %reduce-scatter.2.cloned.1.call-done = bf16[128,4608]{1,0:T(8,128)(2,1)} async-done(((bf16[512,4608]{1,0:T(8,128)(2,1)}), bf16[128,4608]{1,0:T(8,128)(2,1)}) %reduce-scatter.2.cloned.1.call-update) | async-done | bytes 1179664 | tf_op jit(solution)/shard_map/reduce_scatter | solution.py:163
  387.1 1.6 fusion.5
  388.7 2.8 fusion.9
  (23 shorter events, 0.3 us)
Async XLA Ops:
  6.5 169.4 %copy-start = (s32[32,32]{1,0:T(8,128)S(1)}, s32[32,32]{1,0:T(8,128)}, u32[]{:S(2)}) copy-start(s32[32,32]{1,0:T(8,128)} %param.15) | copy-start | bytes 12292
  6.5 61.4 %all-gather.9.cloned.1.call-start = ((), (), s32[]{:S(2)}) async-start(), calls=%async_computation.4 | async-start | bytes 5898240 | tf_op jit(solution)/shard_map/all_gather | solution.py:126
  7.3 143.1 %all-gather.5.cloned.1.call-start = ((), (), s32[]{:S(2)}) async-start(), calls=%async_computation.1 | async-start | bytes 4866048 | tf_op jit(solution)/shard_map/all_gather | solution.py:142
  8.9 292.9 %all-gather.7.cloned.1.call-start = ((), (), s32[]{:S(2)}) async-start(), calls=%async_computation.2 | async-start | bytes 17301504 | tf_op jit(solution)/shard_map/all_gather | solution.py:154
  157.9 7.1 %collective-permute-start = (bf16[512,2,256]{0,2,1:T(8,128)(2,1)S(1)}, bf16[512,2,256]{0,2,1:T(8,128)(2,1)S(1)}, u32[]{:S(2)}, u32[]{:S(2)}) collective-permute-start(bf16[512,2,256]{0,2,1:T(8,128)(2,1)S(1)} %pad_maximum_fusion), channel_id=1, source_target_pairs={{0,128},{1,129},{2,130},{3,131},{4,132},{5,133},{6,134},{7,135},{8... | collective-permute-start | bytes 1572872 | tf_op jit(solution)/shard_map/ppermute | solution.py:25
  166.0 221.1 %reduce-scatter.2.cloned.1.call-start = ((), (), s32[]{:S(2)}) async-start(), calls=%async_computation.3 | async-start | bytes 5898240 | tf_op jit(solution)/shard_map/reduce_scatter | solution.py:163
  183.2 125.1 %slice-start = ((s8[4718592]{0:T(1024)(128)(4,1)}), s8[524288]{0:T(1024)(128)(4,1)S(1)}, s32[]{:S(2)}) async-start(s8[4718592]{0:T(1024)(128)(4,1)} %bitcast.41), calls=%async_computation.5 | async-start | bytes 1048576
  302.6 5.7 %slice-start.1 = ((s8[4718592]{0:T(1024)(128)(4,1)}), s8[4194304]{0:T(1024)(128)(4,1)S(1)}, s32[]{:S(2)}) async-start(s8[4718592]{0:T(1024)(128)(4,1)} %bitcast.41), calls=%async_computation.6 | async-start | bytes 8388608
  313.6 0.7 copy-start.2
  313.6 75.1 %copy-start.1 = (bf16[1,128,4608]{2,1,0:T(8,128)(2,1)S(1)}, bf16[1,128,4608]{2,1,0:T(8,128)(2,1)}, u32[]{:S(2)}) copy-start(bf16[1,128,4608]{2,1,0:T(8,128)(2,1)} %param.8) | copy-start | bytes 3538948
Sparse Core Ops, SparseCore 0:
  9.1 58.7 all-gather.8
  70.5 79.8 all-gather.4
  166.2 135.5 all-gather.6
  313.7 73.3 reduce-scatter.1

commit v2 on v1

v2 whole, which is shorter than its diff:
```python
import math

import functools

import jax
import jax.numpy as jnp
from jax import lax
from jax.experimental import pallas as pl
from jax.experimental.pallas import tpu as pltpu
from jax.sharding import PartitionSpec as P

HEAD_WIDTH = 128


epsilon = 1e-06
softcap_limit = 50.0
query_scale = 144.0 ** (-0.5)
RAISE = softcap_limit * math.log2(math.e)
XS, ZS = 4, 8


def normalize(values):
    return values * lax.rsqrt(jnp.mean(values * values, axis=-1, keepdims=True) + epsilon)


def apply_rotation(values, token_positions):
    half_size = values.shape[-1] // 2
    frequency = 10000.0 ** (-(jnp.arange(half_size, dtype=jnp.float32) * 2.0 / values.shape[-1]))
    angles = token_positions.astype(jnp.float32)[:, None] * frequency[None, :]
    cosine = jnp.cos(angles)[:, None, :]
    sine_part = jnp.sin(angles)[:, None, :]
    first_half = values[..., :half_size]
    second_half = values[..., half_size:]
    return jnp.concatenate(
        [
            first_half * cosine - second_half * sine_part,
            second_half * cosine + first_half * sine_part,
        ],
        axis=-1,
    )


SLOTS = ((0, 0), (1, 0), (1, 1), (1, 3), (2, 0), (1, 2), (2, 1), (2, 3), (3, 0), (2, 2), (3, 1), (3, 3), (4, 0), (3, 2), (-1, 1), (-1, 3), (-1, 2))


def start_copy(source, target, sent, landed, **place):
    copy = pltpu.make_async_remote_copy(
        src_ref=source,
        dst_ref=target,
        send_sem=sent,
        recv_sem=landed,
        device_id=place,
        device_id_type=pl.DeviceIdType.MESH,
    )
    return copy


def greet(places):
    barrier = pltpu.get_barrier_semaphore()
    for place in places:
        pl.semaphore_signal(
            barrier, inc=1, device_id=place, device_id_type=pl.DeviceIdType.MESH
        )
    pl.semaphore_wait(barrier, len(places))


def attention_kernel(
    meta, q_ref, kv_ref, start_ref, out_ref,
    queries, blocks, total, wide, ready, landing,
    swap_s, swap_r, own_s, z_s, z_r, right_s, right_r, left_s, left_r, key_s, key_r, value_s, value_r, far_s, far_r,
):
    section = lax.axis_index("section")
    shard = lax.axis_index("seq")
    z, x = shard // XS, shard % XS
    other = 1 - section
    rows = start_ref.shape[0]
    up = ((z + 1) % ZS) * XS + x
    down = ((z + ZS - 1) % ZS) * XS + x
    right = z * XS + (x + 1) % XS
    left = z * XS + (x + 3) % XS
    far = z * XS + (x + 2) % XS
    greet([{"section": other}, {"seq": up}, {"seq": down}, {"seq": right}, {"seq": left}, {"seq": far}])

    def swap_queries():
        return start_copy(
            q_ref.at[pl.ds(2 * other, 2)], queries.at[pl.ds(2 * section, 2)],
            swap_s.at[0], swap_r.at[0], section=other,
        )

    def hand_keys():
        return start_copy(kv_ref.at[1], blocks.at[0], swap_s.at[1], swap_r.at[1], section=other)

    def climb(step):
        slots = (0, 1, 4, 8, 12)
        return start_copy(
            blocks.at[slots[step]], blocks.at[slots[step + 1]], z_s.at[step], z_r.at[step], seq=up
        )

    def to_right(row):
        source, target = ((1, 2), (4, 6), (8, 10))[row]
        return start_copy(blocks.at[source], blocks.at[target], right_s.at[row], right_r.at[row], seq=right)

    def to_left(row):
        source, target = ((1, 3), (4, 7), (8, 11))[row]
        return start_copy(blocks.at[source], blocks.at[target], left_s.at[row], left_r.at[row], seq=left)

    def pass_keys(row):
        source, target = ((2, 5), (6, 9), (10, 13))[row]
        columns = pl.ds(0, HEAD_WIDTH)
        return start_copy(
            blocks.at[source, :, columns], blocks.at[target, :, columns], key_s.at[row], key_r.at[row], seq=right
        )

    def pass_values(row):
        source, target = ((3, 5), (7, 9), (11, 13))[row]
        columns = pl.ds(HEAD_WIDTH, HEAD_WIDTH)
        return start_copy(
            blocks.at[source, :, columns], blocks.at[target, :, columns], value_s.at[row], value_r.at[row], seq=left
        )

    def edge_right(source):
        return start_copy(blocks.at[source], blocks.at[14], right_s.at[3], right_r.at[3], seq=right)

    def edge_left(source):
        return start_copy(blocks.at[source], blocks.at[15], left_s.at[3], left_r.at[3], seq=left)

    def edge_far(source):
        return start_copy(blocks.at[source], blocks.at[16], far_s.at[0], far_r.at[0], seq=far)

    own_queries = pltpu.make_async_copy(
        q_ref.at[pl.ds(2 * section, 2)], queries.at[pl.ds(2 * section, 2)], own_s.at[0]
    )
    own_keys = pltpu.make_async_copy(kv_ref.at[0], blocks.at[0], own_s.at[1])
    swap_queries().start()
    own_queries.start()

    @pl.when(section == 0)
    def _():
        hand_keys().start()
        own_keys.start()

    total[...] = jnp.zeros_like(total)
    wide[...] = jnp.ones_like(wide)

    @pl.when(section == 0)
    def _():
        own_keys.wait()

    @pl.when(section == 1)
    def _():
        hand_keys().wait_recv()

    climb(0).start()
    pl.when(x < 3)(lambda: edge_right(0).start())
    pl.when(x == 0)(lambda: edge_left(0).start())
    pl.when(x < 2)(lambda: edge_far(0).start())
    own_queries.wait()
    swap_queries().wait_recv()

    def turn(step):
        if step == 1:
            climb(0).wait_recv()
            climb(1).start()
            to_right(0).start()
            to_left(0).start()
        elif step in (2, 6, 10):
            row = (step - 2) // 4
            to_right(row).wait_recv()
            pass_keys(row).start()
            to_left(row).wait_recv()
            pass_values(row).start()
            climb(row + 1).wait_recv()
            if row < 2:
                climb(row + 2).start()
                to_right(row + 1).start()
                to_left(row + 1).start()
            else:
                pl.when(x == 3)(lambda: edge_right(12).start())
                pl.when(x > 0)(lambda: edge_left(12).start())
                pl.when(x > 1)(lambda: edge_far(12).start())
        elif step in (5, 9, 13):
            row = (step - 5) // 4
            pass_keys(row).wait_recv()
            pass_values(row).wait_recv()
        elif step == 14:
            edge_right(0).wait_recv()
        elif step == 15:
            edge_left(0).wait_recv()
        elif step == 16:
            edge_far(0).wait_recv()

    def visit(step, carried):
        for number in (1, 2, 5, 6, 9, 10, 13, 14, 15, 16):
            pl.when(step == number)(functools.partial(turn, number))
        first = meta[0, step]
        listed = meta[1, step] == 1
        start = jnp.where(listed, start_ref[:, :1], shard * rows + rows)
        keys = first + lax.broadcasted_iota(jnp.int32, (rows, rows), 1)
        own = shard * rows + lax.broadcasted_iota(jnp.int32, (rows, rows), 0)
        seen = (keys >= start) & (keys <= own)
        wide[:, :HEAD_WIDTH] = blocks[step, :, HEAD_WIDTH:]
        for head in range(4):
            scores = lax.dot_general(
                queries[head],
                blocks[step, :, :HEAD_WIDTH],
                (((1,), (1,)), ((), ())),
                preferred_element_type=jnp.float32,
            )
            raised = jnp.where(seen, jnp.exp2(jnp.tanh(scores) * RAISE), 0.0)
            total[head] += jnp.dot(
                raised.astype(jnp.bfloat16), wide[...], preferred_element_type=jnp.float32
            )
        return carried

    lax.fori_loop(0, len(SLOTS), visit, 0)

    for mine in range(2):
        value = total[2 * other + mine]
        ready[:, mine * HEAD_WIDTH : (mine + 1) * HEAD_WIDTH] = (
            value[:, :HEAD_WIDTH] / value[:, HEAD_WIDTH:]
        ).astype(jnp.bfloat16)
    swap_back = start_copy(ready, landing, swap_s.at[2], swap_r.at[2], section=other)
    swap_back.start()
    for mine in range(2):
        value = total[2 * section + mine]
        out_ref[section, :, mine * HEAD_WIDTH : (mine + 1) * HEAD_WIDTH] = (
            value[:, :HEAD_WIDTH] / value[:, HEAD_WIDTH:]
        ).astype(jnp.bfloat16)
    swap_back.wait_recv()
    out_ref[other] = landing[...]
    swap_back.wait_send()
    swap_queries().wait_send()
    pl.when(section == 0)(lambda: hand_keys().wait_send())
    for step in range(4):
        climb(step).wait_send()
    for row in range(3):
        to_right(row).wait_send()
        to_left(row).wait_send()
        pass_keys(row).wait_send()
        pass_values(row).wait_send()
    edge_right(0).wait_send()
    edge_left(0).wait_send()
    edge_far(0).wait_send()


def attention(queries, own_kv, starts, meta):
    rows = starts.shape[0]
    dma = pltpu.SemaphoreType.DMA
    whole = pl.BlockSpec(memory_space=pltpu.VMEM)
    return pl.pallas_call(
        attention_kernel,
        out_shape=jax.ShapeDtypeStruct((2, rows, 2 * HEAD_WIDTH), jnp.bfloat16),
        in_specs=[pl.BlockSpec(memory_space=pltpu.SMEM), whole, whole, whole],
        out_specs=whole,
        scratch_shapes=[
            pltpu.VMEM((4, rows, HEAD_WIDTH), jnp.bfloat16),
            pltpu.VMEM((len(SLOTS), rows, 2 * HEAD_WIDTH), jnp.bfloat16),
            pltpu.VMEM((4, rows, 2 * HEAD_WIDTH), jnp.float32),
            pltpu.VMEM((rows, 2 * HEAD_WIDTH), jnp.bfloat16),
            pltpu.VMEM((rows, 2 * HEAD_WIDTH), jnp.bfloat16),
            pltpu.VMEM((rows, 2 * HEAD_WIDTH), jnp.bfloat16),
            dma((3,)), dma((3,)), dma((2,)),
            dma((4,)), dma((4,)), dma((4,)), dma((4,)), dma((4,)), dma((4,)),
            dma((3,)), dma((3,)), dma((3,)), dma((3,)), dma((1,)), dma((1,)),
        ],
        compiler_params=pltpu.CompilerParams(
            collective_id=1, has_side_effects=True, vmem_limit_bytes=56 * 2**20
        ),
        name="attention",
    )(meta, queries, own_kv, starts)


PIECES = 3


def mix_kernel(
    heads_ref, weight_hbm, hidden_ref, gain_ref, out_ref,
    weight, far_out, near_out, sum_out, far_in, near_in, sum_in, mixed,
    load, far_s, far_r, near_s, near_r, sum_s, sum_r,
):
    place = lax.axis_index("head")
    count = 4
    sides = ((place + 1) % count, (place + 3) % count)
    opposite = (place + 2) % count
    rows, width = mixed.shape
    half = width // 2
    piece = half // PIECES
    fetch = pltpu.make_async_copy(weight_hbm, weight, load.at[0])
    fetch.start()
    greet([{"head": sides[0]}, {"head": sides[1]}])
    fetch.wait()
    depth = heads_ref.shape[2]

    def partial(target, low):
        span = pl.ds(pl.multiple_of(target * rows, rows), rows)
        return jnp.dot(
            heads_ref[0, span, :], weight[:depth, low : low + piece], preferred_element_type=jnp.float32
        ) + jnp.dot(
            heads_ref[1, span, :], weight[depth:, low : low + piece], preferred_element_type=jnp.float32
        )

    def send(source, target, sent, landed, side, part):
        return start_copy(
            source.at[side, part], target.at[side, part], sent.at[side, part], landed.at[side, part],
            head=sides[side],
        )

    def far_copy(side, part):
        return send(far_out, far_in, far_s, far_r, side, part)

    def near_copy(side, part):
        return send(near_out, near_in, near_s, near_r, side, part)

    def sum_copy(side, part):
        return send(sum_out, sum_in, sum_s, sum_r, side, part)

    for part in range(PIECES):
        for side in range(2):
            low = side * half + part * piece
            far_out[side, part] = partial(opposite, low).astype(jnp.bfloat16)
            far_copy(side, part).start()
    for part in range(PIECES):
        for side in range(2):
            low = (1 - side) * half + part * piece
            near_out[side, part] = partial(sides[side], low).astype(jnp.bfloat16)
            near_copy(side, part).start()
    for part in range(PIECES):
        for side in range(2):
            low = side * half + part * piece
            own = partial(sides[side], low).astype(jnp.bfloat16).astype(jnp.float32)
            far_copy(side, part).wait_recv()
            sum_out[side, part] = (own + far_in[side, part].astype(jnp.float32)).astype(jnp.bfloat16)
            sum_copy(side, part).start()
    for part in range(2 * PIECES):
        low = part * piece
        mixed[:, low : low + piece] = partial(place, low).astype(jnp.bfloat16).astype(jnp.float32)
    for part in range(PIECES):
        for side in range(2):
            low = (1 - side) * half + part * piece
            near_copy(side, part).wait_recv()
            mixed[:, low : low + piece] += near_in[side, part].astype(jnp.float32)
    squares = jnp.zeros((rows, 128), jnp.float32)
    for part in range(PIECES):
        for side in range(2):
            low = side * half + part * piece
            sum_copy(side, part).wait_recv()
            value = mixed[:, low : low + piece] + sum_in[side, part].astype(jnp.float32)
            mixed[:, low : low + piece] = value
            square = value * value
            for column in range(0, piece, 128):
                squares = squares + square[:, column : column + 128]
    scale = lax.rsqrt(jnp.sum(squares, axis=-1, keepdims=True) / width + epsilon)
    for part in range(2 * PIECES):
        span = slice(part * piece, (part + 1) * piece)
        out_ref[:, span] = (
            hidden_ref[:, span].astype(jnp.float32) + mixed[:, span] * scale * gain_ref[:, span]
        ).astype(jnp.bfloat16)
    for part in range(PIECES):
        for side in range(2):
            far_copy(side, part).wait_send()
            near_copy(side, part).wait_send()
            sum_copy(side, part).wait_send()


def mix(heads, weight, hidden, gain):
    rows, width = hidden.shape
    dma = pltpu.SemaphoreType.DMA
    whole = pl.BlockSpec(memory_space=pltpu.VMEM)
    slots = pltpu.VMEM((2, PIECES, rows, width // (2 * PIECES)), jnp.bfloat16)
    return pl.pallas_call(
        mix_kernel,
        out_shape=jax.ShapeDtypeStruct((rows, width), jnp.bfloat16),
        in_specs=[whole, pl.BlockSpec(memory_space=pl.ANY), whole, whole],
        out_specs=whole,
        scratch_shapes=[
            pltpu.VMEM(weight.shape, jnp.bfloat16),
            slots, slots, slots, slots, slots, slots,
            pltpu.VMEM((rows, width), jnp.float32),
            dma((1,)),
        ]
        + [dma((2, PIECES))] * 6,
        compiler_params=pltpu.CompilerParams(
            collective_id=2, has_side_effects=True, vmem_limit_bytes=56 * 2**20
        ),
        name="mix",
    )(heads, weight, hidden, gain)


def visits(shard, rows, block_table):
    z, x = shard // XS, shard % XS
    back = jnp.array([row for row, _ in SLOTS], jnp.int32)
    aside = jnp.array([column for _, column in SLOTS], jnp.int32)
    source = (x + XS - aside) % XS
    back = jnp.where(back < 0, jnp.where(source < x, 0, 4), back)
    block = (z - back) * XS + source
    listed = block_table[shard][jnp.maximum(block, 0)]
    return jnp.stack([block * rows, listed])


def local(hidden, q_weight, key_value_weight, o_weight, in_gain, post_gain, positions, block_table):
    shard_index = lax.axis_index("seq")
    gathered = lax.all_gather(hidden[0], "head", axis=0, tiled=True)
    local_rows = gathered.shape[0]
    first_row = shard_index * local_rows
    local_positions = lax.dynamic_slice_in_dim(positions, first_row, local_rows)
    normed = (normalize(gathered.astype(jnp.float32)) * in_gain[0]).astype(jnp.bfloat16)
    query_matrix = jnp.dot(normed, q_weight[0], preferred_element_type=jnp.float32)
    head_count = query_matrix.shape[1] // HEAD_WIDTH
    query_matrix = apply_rotation(
        query_matrix.reshape(local_rows, head_count, HEAD_WIDTH), local_positions
    )
    query_matrix = (query_matrix * (query_scale / softcap_limit)).astype(jnp.bfloat16)
    query_matrix = jnp.transpose(query_matrix, (1, 0, 2))
    value_width = key_value_weight.shape[2]
    projected_rows = jnp.einsum(
        "td,dce->tce",
        normed,
        lax.all_gather(key_value_weight, "seq", axis=0, tiled=True),
        preferred_element_type=jnp.float32,
    )
    key_heads = value_width // HEAD_WIDTH
    rotated_keys = apply_rotation(
        projected_rows[:, 0].reshape(local_rows, key_heads, HEAD_WIDTH), local_positions
    )
    own_kv = jnp.stack(
        [
            jnp.concatenate(
                [rotated_keys[:, head], projected_rows[:, 1, head * HEAD_WIDTH : (head + 1) * HEAD_WIDTH]],
                axis=1,
            )
            for head in range(key_heads)
        ]
    ).astype(jnp.bfloat16)
    query_index = first_row + jnp.arange(local_rows, dtype=jnp.int32)
    starts = jnp.broadcast_to((query_index - local_positions)[:, None], (local_rows, HEAD_WIDTH))
    attended = attention(query_matrix, own_kv, starts, visits(shard_index, local_rows, block_table))
    return mix(attended, o_weight[0], hidden[0], post_gain)[None]


def solution(mesh):
    placed = (
        P("section", ("seq", "head"), None),
        P("section", None, "head"),
        P("seq", None, "head"),
        P("section", "head", None),
        P("section", None),
        P("section", None),
        P(),
        P(),
    )
    return jax.shard_map(
        local,
        mesh=mesh,
        in_specs=placed,
        out_specs=P("section", ("seq", "head"), None),
        check_vma=False,
    )
```

time: 399 us -> 289 us (0.72)
  waiting for transfers between devices: 333 us -> 122 us
  Pallas kernels: 5.67 us -> 119 us
  matrix products: 18.7 us -> 12 us
    all_gather x1 -> x0, waiting for transfers between devices: 118 us -> none  [local(): lax.all_gather(shared.reshape(local_rows, -1), 'seq', axis=0, tiled=True)]
    pallas_call x1 -> x2, Pallas kernels: 5.67 us -> 119 us  [the longest x1 71.6 us: attention(): pl.pallas_call(attention_kernel, out_shape=jax.ShapeDtypeStruct((2, rows,...]
    reduce_scatter x1 -> x0, waiting for transfers between devices: 72.8 us -> none  [local(): lax.psum_scatter(jnp.dot(attended, out_proj, preferred_element_type=jnp.f...]
    all_gather x1, waiting for transfers between devices: 56.9 us -> 48.9 us  [local(): gathered = lax.all_gather(hidden[0], 'head', axis=0, tiled=True)]
    all_gather x1, waiting for transfers between devices: 79.1 us -> 72.3 us  [local(): lax.all_gather(key_value_weight, 'seq', axis=0, tiled=True)]
    ppermute x1 -> x0, waiting for transfers between devices: 5.76 us -> none  [shifted(): lax.ppermute(value, axis, [(source, source + steps) for source in range(f...]
    dot_general x1 -> x0, matrix products: 5.31 us -> none  [local(): jnp.dot(attended, out_proj, preferred_element_type=jnp.float32)]
  transfers between devices with their start and end apart: 5 -> 2, of which waited for: 5 -> 2; matrix products, arithmetic and copies ran while one was open for 6% -> 7% of each run, Pallas kernels for 0% -> 0%
where the time goes in v2:
time: 289 us
  waiting for transfers between devices  122 us (42%)
  Pallas kernels  119 us (41%)
  between operations  13.6 us (5%)
  local copies, waits for them, and re-layouts  13.3 us (5%)
  matrix products  12 us (4%)
  other arithmetic  8.76 us (3%)
    all_gather x1, waiting for transfers between devices, local(): lax.all_gather(key_value_weight, 'seq', axis=0, tiled=True)  72.3 us
    pallas_call x1, Pallas kernels, attention(): pl.pallas_call(attention_kernel, out_shape=jax.ShapeDtypeStruct((2, rows,...  71.6 us
    all_gather x1, waiting for transfers between devices, local(): gathered = lax.all_gather(hidden[0], 'head', axis=0, tiled=True)  48.9 us
    pallas_call x1, Pallas kernels, mix(): pl.pallas_call(mix_kernel, out_shape=jax.ShapeDtypeStruct((rows, width),...  47.6 us
    dot_general x1, matrix products, local(): jnp.einsum('td,dce->tce', normed, lax.all_gather(key_value_weight, 'seq',...  7.23 us
    dot_general x1, local copies, waits for them, and re-layouts, local(): jnp.dot(normed, q_weight[0], preferred_element_type=jnp.float32)  6.78 us
  transfers between devices with their start and end apart: 2, of which 2 were waited for; matrix products, arithmetic and copies ran while one was open for 7% of the time, Pallas kernels for 0%

profile of v2, /device:TPU:1, one launch (start us, length us, event | category | flops | bytes accessed | tf_op | source)
XLA Modules:
  0.0 288.8 jit_solution(16867640983118856505)
XLA Ops:
  6.5 0.7 all-gather.6.cloned.1.call-update
  7.3 0.0 all-gather.4.cloned.1.call-start
  7.3 1.6 copy.19
  8.9 0.0 all-gather.4.cloned.1.call-update
  8.9 0.0 copy-start.2
  8.9 0.0 copy-start.3
  8.9 0.0 copy-start.4
  9.0 0.0 copy-start.5
  9.0 6.8 %copy.24 = bf16[512,4608]{1,0:T(8,128)(2,1)} copy(bf16[512,4608]{0,1:T(8,128)(2,1)} %bitcast.39) | data formatting | bytes 9437184 | tf_op jit(solution)/shard_map/dot_general | solution.py:407
  15.9 0.7 gather_fusion
  16.6 0.6 pad_add_fusion.meta
  17.2 0.8 add_subtract_fusion
  18.0 1.0 multiply_cosine_fusion
  19.0 48.9 %all-gather.6.cloned.1.call-done = bf16[1,512,4608]{2,1,0:T(8,128)(2,1)} async-done(((bf16[1,128,4608]{2,1,0:T(8,128)(2,1)}), bf16[1,512,4608]{2,1,0:T(8,128)(2,1)}) %all-gather.6.cloned.1.call-update) | async-done | bytes 4718608 | tf_op jit(solution)/shard_map/all_gather | solution.py:402
  67.9 3.5 %fusion = f32[512]{0:T(512)S(1)} fusion(bf16[1,512,4608]{2,1,0:T(8,128)(2,1)} %all-gather.6.cloned.1.call-done), kind=kLoop, calls=%fused_computation.3 | loop fusion | flops 7077376 | bytes 4720640 | tf_op jit(solution)/shard_map/reduce_sum | solution.py:23
  71.4 0.3 copy-done.1
  71.7 4.8 %fusion.8 = f32[512,4,128]{2,0,1:T(8,128)S(1)} fusion(bf16[4,128,4608]{2,1,0:T(8,128)(2,1)} %bitcast.41, bf16[1,512,4608]{2,1,0:T(8,128)(2,1)S(1)} %copy-done.1, f32[4608]{0:T(1024)S(1)} %reduce, f32[512]{0:T(512)S(1)} %add_rsqrt_fusion), kind=kOutput, calls=%fused_computation.21 | convolution fusion | flops 2425356288 | bytes 10506240 | tf_op jit(solution)/shard_map/dot_general | solution.py:407
  76.5 0.5 multiply_subtract_fusion
  77.0 1.1 fusion.5.q_ref
  78.1 72.3 %all-gather.4.cloned.1.call-done = bf16[4608,2,256]{2,0,1:T(8,128)(2,1)} async-done(((bf16[144,2,256]{2,0,1:T(8,128)(2,1)}), bf16[4608,2,256]{2,0,1:T(8,128)(2,1)}) %all-gather.4.cloned.1.call-update) | async-done | bytes 4718608 | tf_op jit(solution)/shard_map/all_gather | solution.py:418
  150.4 7.2 %fusion.6 = f32[512,2,256]{0,2,1:T(8,128)S(1)} fusion(bf16[4608,2,256]{2,0,1:T(8,128)(2,1)} %all-gather.4.cloned.1.call-done, bf16[1,512,4608]{2,1,0:T(8,128)(2,1)} %all-gather.6.cloned.1.call-done, f32[4608]{0:T(1024)S(1)} %reduce, f32[512]{0:T(512)S(1)} %add_rsqrt_fusion), kind=kOutput, calls=%fused_computation.20 | convolution fusion | flops 2425356288 | bytes 10506240 | tf_op jit(solution)/shard_map/td,dce->tce/dot_general | solution.py:415
  157.7 0.2 copy.22
  157.9 0.2 copy.25
  158.1 0.2 copy.26
  158.3 0.1 multiply_subtract_fusion.1
  158.5 0.1 maximum_convert_fusion
  158.7 0.1 maximum_bitcast_fusion
  158.8 0.8 pad_maximum_fusion.kv_ref
  159.6 0.8 broadcast_in_dim.9.start_ref
  160.5 71.6 %attention.1.heads_ref = bf16[2,512,256]{2,1,0:T(8,128)(2,1)} custom-call(s32[2,17]{1,0:T(2,128)} %pad_add_fusion.meta, bf16[4,512,128]{2,1,0:T(8,128)(2,1)} %fusion.5.q_ref, bf16[2,512,256]{2,1,0:T(8,128)(2,1)} %pad_maximum_fusion.kv_ref, s32[512,128]{1,0:T(8,128)} %broadcast_in_dim.9.start_ref), custom_call_target="tpu_custom_call" | custom-call | tf_op jit(solution)/shard_map/attention/pallas_call | solution.py:250
  232.0 47.6 %mix.1 = bf16[128,4608]{1,0:T(8,128)(2,1)} custom-call(bf16[2,512,256]{2,1,0:T(8,128)(2,1)} %attention.1.heads_ref, bf16[512,4608]{1,0:T(8,128)(2,1)} %bitcast.40, bf16[128,4608]{1,0:T(8,128)(2,1)} %bitcast.42, f32[1,4608]{1,0:T(1,128)} %gain_ref.1), custom_call_target="tpu_custom_call" | custom-call | tf_op jit(solution)/shard_map/mix/pallas_call | solution.py:370
  279.6 2.4 copy.28
  (19 shorter events, 0.2 us)
Async XLA Ops:
  6.5 9.3 %copy-start = (s32[32,32]{1,0:T(8,128)S(1)}, s32[32,32]{1,0:T(8,128)}, u32[]{:S(2)}) copy-start(s32[32,32]{1,0:T(8,128)} %param.17) | copy-start | bytes 12292
  6.5 61.4 %all-gather.6.cloned.1.call-start = ((), (), s32[]{:S(2)}) async-start(), calls=%async_computation.1 | async-start | bytes 5898240 | tf_op jit(solution)/shard_map/all_gather | solution.py:402
  7.3 143.1 %all-gather.4.cloned.1.call-start = ((), (), s32[]{:S(2)}) async-start(), calls=%async_computation | async-start | bytes 4866048 | tf_op jit(solution)/shard_map/all_gather | solution.py:418
  8.9 6.8 %copy-start.2 = (f32[1,4608]{1,0:T(1,128)S(1)}, f32[1,4608]{1,0:T(1,128)}, u32[]{:S(2)}) copy-start(f32[1,4608]{1,0:T(1,128)} %param.14) | copy-start | bytes 55300
  8.9 6.9 %copy-start.3 = (s32[17]{0:T(128)S(1)}, s32[17]{0:T(128)}, u32[]{:S(2)}) copy-start(s32[17]{0:T(128)} %constant.72.clone) | copy-start | bytes 208
  8.9 6.9 %copy-start.4 = (pred[17]{0:T(512)(128)(4,1)S(1)}, pred[17]{0:T(512)(128)(4,1)}, u32[]{:S(2)}) copy-start(pred[17]{0:T(512)(128)(4,1)} %constant.80) | copy-start | bytes 55
  9.0 6.9 %copy-start.5 = (s32[17]{0:T(128)S(1)}, s32[17]{0:T(128)}, u32[]{:S(2)}) copy-start(s32[17]{0:T(128)} %constant.81) | copy-start | bytes 208
  67.9 3.8 %copy-start.1 = (bf16[1,512,4608]{2,1,0:T(8,128)(2,1)S(1)}, bf16[1,512,4608]{2,1,0:T(8,128)(2,1)}, u32[]{:S(2)}) copy-start(bf16[1,512,4608]{2,1,0:T(8,128)(2,1)} %all-gather.6.cloned.1.call-done) | copy-start | bytes 14155780
Sparse Core Ops, SparseCore 0:
  9.1 58.7 all-gather.5
  70.5 79.8 all-gather.3

commit v3 on v2

--- a/solution.py
+++ b/solution.py
@@ -17,27 +17,6 @@
 query_scale = 144.0 ** (-0.5)
 RAISE = softcap_limit * math.log2(math.e)
 XS, ZS = 4, 8
-
-
-def normalize(values):
-    return values * lax.rsqrt(jnp.mean(values * values, axis=-1, keepdims=True) + epsilon)
-
-
-def apply_rotation(values, token_positions):
-    half_size = values.shape[-1] // 2
-    frequency = 10000.0 ** (-(jnp.arange(half_size, dtype=jnp.float32) * 2.0 / values.shape[-1]))
-    angles = token_positions.astype(jnp.float32)[:, None] * frequency[None, :]
-    cosine = jnp.cos(angles)[:, None, :]
-    sine_part = jnp.sin(angles)[:, None, :]
-    first_half = values[..., :half_size]
-    second_half = values[..., half_size:]
-    return jnp.concatenate(
-        [
-            first_half * cosine - second_half * sine_part,
-            second_half * cosine + first_half * sine_part,
-        ],
-        axis=-1,
-    )
 
 
 SLOTS = ((0, 0), (1, 0), (1, 1), (1, 3), (2, 0), (1, 2), (2, 1), (2, 3), (3, 0), (2, 2), (3, 1), (3, 3), (4, 0), (3, 2), (-1, 1), (-1, 3), (-1, 2))
@@ -386,6 +365,200 @@
     )(heads, weight, hidden, gain)
 
 
+def project_kernel(
+    hidden_ref, gain_ref, cos_ref, sin_ref, query_hbm, share_ref, q_out, kv_out,
+    normed, query_weight, kv_weight,
+    load, side_s, side_r, x_s, x_r, z_s, z_r,
+):
+    section = lax.axis_index("section")
+    shard = lax.axis_index("seq")
+    place = lax.axis_index("head")
+    z, x = shard // XS, shard % XS
+    up = ((z + 1) % ZS) * XS + x
+    down = ((z + ZS - 1) % ZS) * XS + x
+    rows, width = hidden_ref.shape
+    half = width // 2
+    piece = half // PIECES
+    depth = share_ref.shape[0]
+    sides = ((place + 1) % 4, (place + 3) % 4)
+    across = [z * XS + (x + step) % XS for step in (1, 3, 2)]
+    fetch = pltpu.make_async_copy(query_hbm, query_weight, load.at[0])
+    fetch.start()
+    greet([{"head": sides[0]}, {"head": sides[1]}] + [{"seq": seq} for seq in across + [up, down]])
+
+    def weight_rows(zz, xx):
+        return pl.ds(pl.multiple_of((zz * XS + xx) * depth, 16), depth)
+
+    def share_across(number):
+        return start_copy(
+            share_ref, kv_weight.at[weight_rows(z, x)], x_s.at[number], x_r.at[number], seq=across[number]
+        )
+
+    def climb(side, hop, aside):
+        back = hop - 1
+        origin = (z + ZS - back) % ZS if side == 0 else (z + back) % ZS
+        span = weight_rows(origin, (x + aside) % XS)
+        source = share_ref if hop == 1 and aside == 0 else kv_weight.at[span]
+        return start_copy(
+            source, kv_weight.at[span], z_s.at[side, hop - 1, aside], z_r.at[side, hop - 1, aside],
+            seq=(up, down)[side],
+        )
+
+    climbs = [
+        (side, hop, aside)
+        for hop in range(1, 5)
+        for aside in range(4)
+        for side in range(2)
+        if hop < 4 or (aside < 2) == (side == 0)
+    ]
+
+    def row_copy(side, kind, part):
+        which = side if kind == 0 else 1 - side
+        span = pl.ds((side if kind == 2 else which) * half + part * piece, piece)
+        source = (0, 0, 1 + side)[kind]
+        target = (1 + side, 1 + side, 3)[kind]
+        return start_copy(
+            normed.at[source, :, span], normed.at[target, :, span],
+            side_s.at[side, kind, part], side_r.at[side, kind, part], head=sides[side],
+        )
+
+    @pl.when(section == 0)
+    def _():
+        for number in range(3):
+            share_across(number).start()
+        for side in range(2):
+            climb(side, 1, 0).start()
+        kv_weight[weight_rows(z, x), :] = share_ref[...]
+
+    squares = jnp.zeros((rows, 128), jnp.float32)
+    for column in range(0, width, 128):
+        value = hidden_ref[:, column : column + 128].astype(jnp.float32)
+        squares = squares + value * value
+    scale = lax.rsqrt(jnp.sum(squares, axis=-1, keepdims=True) / width + epsilon)
+    for part in range(2 * PIECES):
+        span = slice(part * piece, (part + 1) * piece)
+        normed[0, :, span] = (
+            hidden_ref[:, span].astype(jnp.float32) * scale * gain_ref[:, span]
+        ).astype(jnp.bfloat16)
+    for kind in range(2):
+        for part in range(PIECES):
+            for side in range(2):
+                row_copy(side, kind, part).start()
+
+    @pl.when(section == 0)
+    def _():
+        for number, aside in ((0, 3), (1, 1), (2, 2)):
+            share_across(number).wait_recv()
+            for side in range(2):
+                climb(side, 1, aside).start()
+
+    steps = (0, 3, 1, 2)
+
+    def product(first, count, weight, low):
+        return jnp.dot(
+            normed[first : first + count].reshape(count * rows, width),
+            weight[:, low : low + 2 * HEAD_WIDTH],
+            preferred_element_type=jnp.float32,
+        )
+
+    def token_rows(slot):
+        return pl.ds(pl.multiple_of(((place + steps[slot]) % 4) * rows, rows), rows)
+
+    def turned(value, span):
+        return value * cos_ref[span, :] + pltpu.roll(value, HEAD_WIDTH // 2, 1) * sin_ref[span, :]
+
+    def make_queries(first, count):
+        for pair in range(2):
+            result = product(first, count, query_weight, pair * 2 * HEAD_WIDTH)
+            for slot in range(count):
+                span = token_rows(first + slot)
+                for mine in range(2):
+                    value = result[slot * rows : (slot + 1) * rows, mine * HEAD_WIDTH : (mine + 1) * HEAD_WIDTH]
+                    q_out[2 * pair + mine, span, :] = (
+                        turned(value, span) * (query_scale / softcap_limit)
+                    ).astype(jnp.bfloat16)
+
+    def make_keys(first, count):
+        for pair in range(2):
+            result = product(first, count, kv_weight, pair * 2 * HEAD_WIDTH)
+            for slot in range(count):
+                span = token_rows(first + slot)
+                for mine in range(2):
+                    value = result[slot * rows : (slot + 1) * rows, mine * HEAD_WIDTH : (mine + 1) * HEAD_WIDTH]
+                    if pair == 0:
+                        value = turned(value, span)
+                    kv_out[mine, span, pair * HEAD_WIDTH : (pair + 1) * HEAD_WIDTH] = value.astype(jnp.bfloat16)
+
+    def pass_weights(hop):
+        @pl.when(section == 0)
+        def _():
+            for side, at, aside in climbs:
+                if at == hop:
+                    climb(side, hop, aside).wait_recv()
+                    if (side, hop + 1, aside) in climbs:
+                        climb(side, hop + 1, aside).start()
+
+    fetch.wait()
+    make_queries(0, 1)
+    pass_weights(1)
+    pass_weights(2)
+    for part in range(PIECES):
+        for side in range(2):
+            row_copy(side, 0, part).wait_recv()
+            row_copy(side, 2, part).start()
+    pass_weights(3)
+    for part in range(PIECES):
+        for side in range(2):
+            row_copy(side, 1, part).wait_recv()
+    make_queries(1, 2)
+    pass_weights(4)
+    pl.when(section == 0)(lambda: make_keys(0, 3))
+    for part in range(PIECES):
+        for side in range(2):
+            row_copy(side, 2, part).wait_recv()
+    pl.when(section == 0)(lambda: make_keys(3, 1))
+    make_queries(3, 1)
+    for side in range(2):
+        for kind in range(3):
+            for part in range(PIECES):
+                row_copy(side, kind, part).wait_send()
+
+    @pl.when(section == 0)
+    def _():
+        for number in range(3):
+            share_across(number).wait_send()
+        for at in climbs:
+            climb(*at).wait_send()
+
+
+def project(hidden, gain, cosine, sine, query_weight, share):
+    rows, width = hidden.shape
+    tokens = cosine.shape[0]
+    columns = query_weight.shape[1]
+    dma = pltpu.SemaphoreType.DMA
+    whole = pl.BlockSpec(memory_space=pltpu.VMEM)
+    return pl.pallas_call(
+        project_kernel,
+        out_shape=(
+            jax.ShapeDtypeStruct((4, tokens, HEAD_WIDTH), jnp.bfloat16),
+            jax.ShapeDtypeStruct((2, tokens, 2 * HEAD_WIDTH), jnp.bfloat16),
+        ),
+        in_specs=[whole, whole, whole, whole, pl.BlockSpec(memory_space=pl.ANY), whole],
+        out_specs=(whole, whole),
+        scratch_shapes=[
+            pltpu.VMEM((4, rows, width), jnp.bfloat16),
+            pltpu.VMEM((width, columns), jnp.bfloat16),
+            pltpu.VMEM((width, share.shape[1]), jnp.bfloat16),
+            dma((1,)),
+            dma((2, 3, PIECES)), dma((2, 3, PIECES)), dma((3,)), dma((3,)), dma((2, 4, 4)), dma((2, 4, 4)),
+        ],
+        compiler_params=pltpu.CompilerParams(
+            collective_id=3, has_side_effects=True, vmem_limit_bytes=56 * 2**20
+        ),
+        name="project",
+    )(hidden, gain, cosine, sine, query_weight, share)
+
+
 def visits(shard, rows, block_table):
     z, x = shard // XS, shard % XS
     back = jnp.array([row for row, _ in SLOTS], jnp.int32)
@@ -398,42 +571,20 @@
 
 
 def local(hidden, q_weight, key_value_weight, o_weight, in_gain, post_gain, positions, block_table):
-    shard_index = lax.axis_index("seq")
-    gathered = lax.all_gather(hidden[0], "head", axis=0, tiled=True)
-    local_rows = gathered.shape[0]
-    first_row = shard_index * local_rows
-    local_positions = lax.dynamic_slice_in_dim(positions, first_row, local_rows)
-    normed = (normalize(gathered.astype(jnp.float32)) * in_gain[0]).astype(jnp.bfloat16)
-    query_matrix = jnp.dot(normed, q_weight[0], preferred_element_type=jnp.float32)
-    head_count = query_matrix.shape[1] // HEAD_WIDTH
-    query_matrix = apply_rotation(
-        query_matrix.reshape(local_rows, head_count, HEAD_WIDTH), local_positions
+    shard = lax.axis_index("seq")
+    tokens = 4 * hidden.shape[1]
+    first = shard * tokens
+    at = lax.dynamic_slice_in_dim(positions, first, tokens)
+    lane = jnp.arange(HEAD_WIDTH, dtype=jnp.int32)
+    frequency = 10000.0 ** (-((lane % (HEAD_WIDTH // 2)).astype(jnp.float32) * 2.0 / HEAD_WIDTH))
+    angles = at.astype(jnp.float32)[:, None] * frequency[None, :]
+    sine = jnp.sin(angles) * jnp.where(lane < HEAD_WIDTH // 2, -1.0, 1.0)
+    share = key_value_weight.reshape(key_value_weight.shape[0], -1)
+    queries, own_kv = project(hidden[0], in_gain, jnp.cos(angles), sine, q_weight[0], share)
+    starts = jnp.broadcast_to(
+        (first + jnp.arange(tokens, dtype=jnp.int32) - at)[:, None], (tokens, HEAD_WIDTH)
     )
-    query_matrix = (query_matrix * (query_scale / softcap_limit)).astype(jnp.bfloat16)
-    query_matrix = jnp.transpose(query_matrix, (1, 0, 2))
-    value_width = key_value_weight.shape[2]
-    projected_rows = jnp.einsum(
-        "td,dce->tce",
-        normed,
-        lax.all_gather(key_value_weight, "seq", axis=0, tiled=True),
-        preferred_element_type=jnp.float32,
-    )
-    key_heads = value_width // HEAD_WIDTH
-    rotated_keys = apply_rotation(
-        projected_rows[:, 0].reshape(local_rows, key_heads, HEAD_WIDTH), local_positions
-    )
-    own_kv = jnp.stack(
-        [
-            jnp.concatenate(
-                [rotated_keys[:, head], projected_rows[:, 1, head * HEAD_WIDTH : (head + 1) * HEAD_WIDTH]],
-                axis=1,
-            )
-            for head in range(key_heads)
-        ]
-    ).astype(jnp.bfloat16)
-    query_index = first_row + jnp.arange(local_rows, dtype=jnp.int32)
-    starts = jnp.broadcast_to((query_index - local_positions)[:, None], (local_rows, HEAD_WIDTH))
-    attended = attention(query_matrix, own_kv, starts, visits(shard_index, local_rows, block_table))
+    attended = attention(queries, own_kv, starts, visits(shard, tokens, block_table))
     return mix(attended, o_weight[0], hidden[0], post_gain)[None]
 
 

time: 289 us -> 179 us (0.62)
  waiting for transfers between devices: 122 us -> 0 us
  Pallas kernels: 119 us -> 168 us
  between operations: 13.6 us -> 0.04 us
  matrix products: 12 us -> 0 us
  local copies, waits for them, and re-layouts: 13.3 us -> 6.2 us
  other arithmetic: 8.76 us -> 3.89 us
    all_gather x2 -> x0, waiting for transfers between devices: 121 us -> none  [the longest x1 72.3 us: local(): lax.all_gather(key_value_weight, 'seq', axis=0, tiled=True)]
    pallas_call x0 -> x1, Pallas kernels: none -> 52.1 us  [project(): pl.pallas_call(project_kernel, out_shape=(jax.ShapeDtypeStruct((4, tokens...]
    dot_general x2 -> x0, matrix products: 12 us -> none  [the longest x1 7.23 us: local(): jnp.einsum('td,dce->tce', normed, lax.all_gather(key_value_weight, 'seq',...]
    dot_general x2 -> x0, local copies, waits for them, and re-layouts: 6.99 us -> none  [the longest x1 6.78 us: local(): jnp.dot(normed, q_weight[0], preferred_element_type=jnp.float32)]
    reduce_sum x1 -> x0, other arithmetic: 3.48 us -> none  [normalize(): jnp.mean(values * values, axis=-1, keepdims=True) + epsilon]
  transfers between devices with their start and end apart: 2 -> 0, of which waited for: 2 -> 0; matrix products, arithmetic and copies ran while one was open for 7% -> 0% of each run, Pallas kernels for 0% -> 0%
where the time goes in v3:
time: 179 us; the launch traced here: 178 us
  Pallas kernels  168 us (94%)
  local copies, waits for them, and re-layouts  6.2 us (3%)
  other arithmetic  3.89 us (2%)
    pallas_call x1, Pallas kernels, attention(): pl.pallas_call(attention_kernel, out_shape=jax.ShapeDtypeStruct((2, rows,...  70.6 us
    pallas_call x1, Pallas kernels, project(): pl.pallas_call(project_kernel, out_shape=(jax.ShapeDtypeStruct((4, tokens...  52.1 us
    pallas_call x1, Pallas kernels, mix(): pl.pallas_call(mix_kernel, out_shape=jax.ShapeDtypeStruct((rows, width),...  45.2 us
    unnamed x4, local copies, waits for them, and re-layouts  4.66 us

profile of v3, /device:TPU:1, one launch (start us, length us, event | category | flops | bytes accessed | tf_op | source)
XLA Modules:
  0.0 178.1 jit_solution(90969920160725335)
XLA Ops:
  0.0 0.0 copy-start
  0.0 0.7 copy-done
  0.7 0.7 multiply_bitcast_fusion
  1.5 0.8 add_subtract_fusion
  2.2 0.7 gather_fusion
  2.9 0.6 pad_add_fusion.meta
  3.5 1.6 copy.11
  5.1 0.8 broadcast_in_dim.30.start_ref
  5.9 1.8 %fusion = (f32[512,128]{1,0:T(8,128)}, f32[512,128]{1,0:T(8,128)}) fusion(f32[128]{0:T(128)S(1)} %get-tuple-element.15, f32[128]{0:T(128)S(1)} %get-tuple-element.16, f32[512]{0:T(512)S(1)} %get-tuple-element.12), kind=kLoop, calls=%fused_computation.3 | loop fusion | flops 131072 | bytes 527360 | tf_op jit(solution)/shard_map/mul | solution.py:581
  7.7 52.1 %project.1 = (bf16[4,512,128]{2,1,0:T(8,128)(2,1)}, bf16[2,512,256]{2,1,0:T(8,128)(2,1)}) custom-call(bf16[128,4608]{1,0:T(8,128)(2,1)} %bitcast.14, f32[1,4608]{1,0:T(1,128)} %gain_ref.2, f32[512,128]{1,0:T(8,128)} %get-tuple-element.14.cos_ref, f32[512,128]{1,0:T(8,128)} %get-tuple-element.13.sin_ref, bf16[4608,512]{1,0:T(8,128)(2,1)} %bitcast.11, ...), custom_call_target="tpu_custom_call" | custom-call | tf_op jit(solution)/shard_map/project/pallas_call | solution.py:540
  59.9 70.6 %attention.1.heads_ref = bf16[2,512,256]{2,1,0:T(8,128)(2,1)} custom-call(s32[2,17]{1,0:T(2,128)} %pad_add_fusion.meta, bf16[4,512,128]{2,1,0:T(8,128)(2,1)} %get-tuple-element.7.q_ref, bf16[2,512,256]{2,1,0:T(8,128)(2,1)} %get-tuple-element.8.kv_ref, s32[512,128]{1,0:T(8,128)} %broadcast_in_dim.30.start_ref), custom_call_target="tpu_custom_call" | custom-call | tf_op jit(solution)/shard_map/attention/pallas_call | solution.py:229
  130.5 45.2 %mix.1 = bf16[128,4608]{1,0:T(8,128)(2,1)} custom-call(bf16[2,512,256]{2,1,0:T(8,128)(2,1)} %attention.1.heads_ref, bf16[512,4608]{1,0:T(8,128)(2,1)} %bitcast.12, bf16[128,4608]{1,0:T(8,128)(2,1)} %bitcast.15, f32[1,4608]{1,0:T(1,128)} %gain_ref.3), custom_call_target="tpu_custom_call" | custom-call | tf_op jit(solution)/shard_map/mix/pallas_call | solution.py:349
  175.8 2.4 %copy.13 = bf16[1,128,4608]{2,1,0:T(8,128)(2,1)} copy(bf16[1,128,4608]{2,1,0:T(8,128)(2,1)} %bitcast.13) | data formatting | bytes 2359296
  (4 shorter events, 0.0 us)
Async XLA Ops:
  0.0 0.7 copy-start

commit v4 on v2

v4 whole, which is shorter than its diff:
```python
import math

import functools

import jax
import jax.numpy as jnp
from jax import lax
from jax.experimental import pallas as pl
from jax.experimental.pallas import tpu as pltpu
from jax.sharding import PartitionSpec as P

HEAD_WIDTH = 128


epsilon = 1e-06
softcap_limit = 50.0
query_scale = 144.0 ** (-0.5)
RAISE = softcap_limit * math.log2(math.e)
XS, ZS = 4, 8


SLOTS = (
    (0, 0), (1, 0), (2, 0), (1, 1), (1, 3), (3, 0), (4, 0), (2, 1), (2, 3),
    (1, 2), (3, 1), (3, 3), (-1, 1), (-1, 3), (2, 2), (3, 2), (-1, 2),
)
PARTS = ((0, 384), (384, 128))
PIECES = 3


def start_copy(source, target, sent, landed, **place):
    copy = pltpu.make_async_remote_copy(
        src_ref=source,
        dst_ref=target,
        send_sem=sent,
        recv_sem=landed,
        device_id=place,
        device_id_type=pl.DeviceIdType.MESH,
    )
    return copy


def greet(places):
    barrier = pltpu.get_barrier_semaphore()
    for place in places:
        pl.semaphore_signal(
            barrier, inc=1, device_id=place, device_id_type=pl.DeviceIdType.MESH
        )
    pl.semaphore_wait(barrier, len(places))


def layer_kernel(
    table, hidden_ref, gain_ref, cos_ref, sin_ref, query_hbm, share_ref, start_ref, out_hbm, post_ref, out_ref,
    meta, normed, query_weight, kv_weight, out_weight, made_queries, made_kv, queries, blocks, starts,
    total, wide, ready, heads, far_out, near_out, sum_out, far_in, near_in, sum_in, mixed,
    load, side_s, side_r, x_s, x_r, w_s, w_r, swap_s, swap_r, own_s, hand_s, hand_r,
    z_s, z_r, right_s, right_r, left_s, left_r, key_s, key_r, value_s, value_r, edge_s, edge_r,
    far_s, far_r, near_s, near_r, sum_s, sum_r,
):
    section = lax.axis_index("section")
    shard = lax.axis_index("seq")
    place = lax.axis_index("head")
    other = 1 - section
    z, x = shard // XS, shard % XS
    up = ((z + 1) % ZS) * XS + x
    down = ((z + ZS - 1) % ZS) * XS + x
    across = [z * XS + (x + step) % XS for step in (1, 3, 2)]
    right, left = across[0], across[1]
    rows, width = hidden_ref.shape
    tokens = start_ref.shape[0]
    half = width // 2
    piece = half // PIECES
    depth = share_ref.shape[0]
    sides = ((place + 1) % 4, (place + 3) % 4)
    steps = (0, 3, 1, 2)
    fetch = pltpu.make_async_copy(query_hbm, query_weight, load.at[0])
    fetch.start()
    fetch_out = pltpu.make_async_copy(out_hbm, out_weight, load.at[1])
    greet(
        [{"head": sides[0]}, {"head": sides[1]}, {"section": other}]
        + [{"seq": seq} for seq in across + [up, down]]
    )

    def weight_rows(zz, xx):
        return pl.ds(pl.multiple_of((zz * XS + xx) * depth, 16), depth)

    def share_across(number):
        return start_copy(
            share_ref, kv_weight.at[weight_rows(z, x)], x_s.at[number], x_r.at[number], seq=across[number]
        )

    def climb_weights(side, hop, aside):
        back = hop - 1
        origin = (z + ZS - back) % ZS if side == 0 else (z + back) % ZS
        span = weight_rows(origin, (x + aside) % XS)
        source = share_ref if hop == 1 and aside == 0 else kv_weight.at[span]
        return start_copy(
            source, kv_weight.at[span], w_s.at[side, hop - 1, aside], w_r.at[side, hop - 1, aside],
            seq=(up, down)[side],
        )

    climbs = [
        (side, hop, aside)
        for hop in range(1, 5)
        for aside in range(4)
        for side in range(2)
        if hop < 4 or (aside < 2) == (side == 0)
    ]

    def row_copy(side, kind, part):
        which = side if kind == 0 else 1 - side
        span = pl.ds((side if kind == 2 else which) * half + part * piece, piece)
        source = (0, 0, 1 + side)[kind]
        target = (1 + side, 1 + side, 3)[kind]
        return start_copy(
            normed.at[source, :, span], normed.at[target, :, span],
            side_s.at[side, kind, part], side_r.at[side, kind, part], head=sides[side],
        )

    def token_rows(slot):
        return pl.ds(pl.multiple_of(((place + steps[slot]) % 4) * rows, rows), rows)

    @pl.when(section == 0)
    def _():
        for number in range(3):
            share_across(number).start()
        for side in range(2):
            climb_weights(side, 1, 0).start()
        kv_weight[weight_rows(z, x), :] = share_ref[...]

    squares = jnp.zeros((rows, 128), jnp.float32)
    for column in range(0, width, 128):
        value = hidden_ref[:, column : column + 128].astype(jnp.float32)
        squares = squares + value * value
    scale = lax.rsqrt(jnp.sum(squares, axis=-1, keepdims=True) / width + epsilon)
    for part in range(2 * PIECES):
        span = slice(part * piece, (part + 1) * piece)
        normed[0, :, span] = (
            hidden_ref[:, span].astype(jnp.float32) * scale * gain_ref[:, span]
        ).astype(jnp.bfloat16)
    for kind in range(2):
        for part in range(PIECES):
            for side in range(2):
                row_copy(side, kind, part).start()

    @pl.when(section == 0)
    def _():
        for number, aside in ((0, 3), (1, 1), (2, 2)):
            share_across(number).wait_recv()
            for side in range(2):
                climb_weights(side, 1, aside).start()

    for number, (back, aside) in enumerate(SLOTS):
        source = (x + XS - aside) % XS
        row = jnp.where(source < x, 0, 4) if back < 0 else back
        block = (z - row) * XS + source
        meta[0, number] = block * tokens
        meta[1, number] = table[shard, jnp.maximum(block, 0)]
    for slot in range(4):
        starts[slot * rows : (slot + 1) * rows, :] = start_ref[token_rows(slot), :]
    total[...] = jnp.zeros_like(total)
    wide[...] = jnp.ones_like(wide)

    def product(first, count, weight, low):
        return jnp.dot(
            normed[first : first + count].reshape(count * rows, width),
            weight[:, low : low + 2 * HEAD_WIDTH],
            preferred_element_type=jnp.float32,
        )

    def turned(value, span):
        return value * cos_ref[span, :] + pltpu.roll(value, HEAD_WIDTH // 2, 1) * sin_ref[span, :]

    def make_queries(first, count):
        for pair in range(2):
            result = product(first, count, query_weight, pair * 2 * HEAD_WIDTH)
            for slot in range(count):
                low = (first + slot) * rows
                for mine in range(2):
                    value = result[slot * rows : (slot + 1) * rows, mine * HEAD_WIDTH : (mine + 1) * HEAD_WIDTH]
                    made_queries[2 * pair + mine, low : low + rows, :] = (
                        turned(value, token_rows(first + slot)) * (query_scale / softcap_limit)
                    ).astype(jnp.bfloat16)

    def make_keys(first, count):
        for pair in range(2):
            result = product(first, count, kv_weight, pair * 2 * HEAD_WIDTH)
            for slot in range(count):
                low = (first + slot) * rows
                for mine in range(2):
                    value = result[slot * rows : (slot + 1) * rows, mine * HEAD_WIDTH : (mine + 1) * HEAD_WIDTH]
                    if pair == 0:
                        value = turned(value, token_rows(first + slot))
                    made_kv[mine, low : low + rows, pair * HEAD_WIDTH : (pair + 1) * HEAD_WIDTH] = value.astype(
                        jnp.bfloat16
                    )

    def pass_weights(hop):
        @pl.when(section == 0)
        def _():
            for side, at, aside in climbs:
                if at == hop:
                    climb_weights(side, hop, aside).wait_recv()
                    if (side, hop + 1, aside) in climbs:
                        climb_weights(side, hop + 1, aside).start()

    def span_of(part):
        return pl.ds(*PARTS[part])

    def hand_keys(part):
        span = span_of(part)
        return start_copy(
            made_kv.at[1, span], blocks.at[0, span], hand_s.at[part], hand_r.at[part], section=other
        )

    def own_keys(part):
        span = span_of(part)
        return pltpu.make_async_copy(made_kv.at[0, span], blocks.at[0, span], own_s.at[1 + part])

    def block_copy(source, target, part, sent, landed, seq, columns=(0, 2 * HEAD_WIDTH)):
        span, width_of = span_of(part), pl.ds(*columns)
        return start_copy(
            blocks.at[source, span, width_of], blocks.at[target, span, width_of], sent, landed, seq=seq
        )

    def climb(step, part):
        slots = (0, 1, 2, 5, 6)
        return block_copy(slots[step], slots[step + 1], part, z_s.at[step, part], z_r.at[step, part], up)

    def to_right(row, part):
        source, target = ((1, 3), (2, 7), (5, 10))[row]
        return block_copy(source, target, part, right_s.at[row, part], right_r.at[row, part], right)

    def to_left(row, part):
        source, target = ((1, 4), (2, 8), (5, 11))[row]
        return block_copy(source, target, part, left_s.at[row, part], left_r.at[row, part], left)

    keys_of, values_of = (0, HEAD_WIDTH), (HEAD_WIDTH, HEAD_WIDTH)

    def pass_keys(row, part):
        source, target = ((3, 9), (7, 14), (10, 15))[row]
        return block_copy(source, target, part, key_s.at[row, part], key_r.at[row, part], right, keys_of)

    def pass_values(row, part):
        source, target = ((4, 9), (8, 14), (11, 15))[row]
        return block_copy(source, target, part, value_s.at[row, part], value_r.at[row, part], left, values_of)

    def edge_right(source, part):
        return block_copy(source, 12, part, right_s.at[3, part], right_r.at[3, part], right)

    def edge_left(source, part):
        return block_copy(source, 13, part, left_s.at[3, part], left_r.at[3, part], left)

    def edge_far(kind, part):
        return block_copy(
            (12, 12, 13, 13)[kind], 16, part, edge_s.at[kind, part], edge_r.at[kind % 2, part],
            (right, right, left, left)[kind], (keys_of, values_of)[kind % 2],
        )

    far_when = (x < 3, x == 2, x == 1, x > 0)

    def begin(part):
        climb(0, part).start()
        pl.when(x < 3)(lambda: edge_right(0, part).start())
        pl.when(x == 0)(lambda: edge_left(0, part).start())

    def climbed(step, part):
        climb(step, part).wait_recv()
        if step < 3:
            climb(step + 1, part).start()
            to_right(step, part).start()
            to_left(step, part).start()
        else:
            pl.when(x == 3)(lambda: edge_right(6, part).start())
            pl.when(x > 0)(lambda: edge_left(6, part).start())

    def spread(row, part):
        to_right(row, part).wait_recv()
        pass_keys(row, part).start()
        to_left(row, part).wait_recv()
        pass_values(row, part).start()

    def passed(row):
        for part in range(2):
            pass_keys(row, part).wait_recv()
            pass_values(row, part).wait_recv()

    def got_right():
        for part in range(2):
            edge_right(0, part).wait_recv()
            for kind in (0, 1):
                pl.when(far_when[kind])(edge_far(kind, part).start)

    def got_left():
        for part in range(2):
            edge_left(0, part).wait_recv()
            for kind in (2, 3):
                pl.when(far_when[kind])(edge_far(kind, part).start)

    fetch.wait()
    make_queries(0, 1)
    pass_weights(1)
    pass_weights(2)
    for part in range(PIECES):
        for side in range(2):
            row_copy(side, 0, part).wait_recv()
            row_copy(side, 2, part).start()
    pass_weights(3)
    for part in range(PIECES):
        for side in range(2):
            row_copy(side, 1, part).wait_recv()
    pass_weights(4)

    @pl.when(section == 0)
    def _():
        make_keys(0, 3)
        hand_keys(0).start()
        own_keys(0).start()
        own_keys(0).wait()

    @pl.when(section == 1)
    def _():
        make_queries(1, 2)
        hand_keys(0).wait_recv()

    begin(0)
    pl.when(section == 0)(lambda: make_queries(1, 2))
    fetch_out.start()
    climbed(0, 0)
    for part in range(PIECES):
        for side in range(2):
            row_copy(side, 2, part).wait_recv()

    @pl.when(section == 0)
    def _():
        make_keys(3, 1)
        hand_keys(1).start()
        own_keys(1).start()
        own_keys(1).wait()

    pl.when(section == 1)(lambda: hand_keys(1).wait_recv())
    begin(1)
    make_queries(3, 1)
    swap_queries = start_copy(
        made_queries.at[pl.ds(2 * other, 2)], queries.at[pl.ds(2 * section, 2)],
        swap_s.at[0], swap_r.at[0], section=other,
    )
    own_queries = pltpu.make_async_copy(
        made_queries.at[pl.ds(2 * section, 2)], queries.at[pl.ds(2 * section, 2)], own_s.at[0]
    )
    swap_queries.start()
    own_queries.start()
    spread(0, 0)
    climbed(1, 0)
    own_queries.wait()
    swap_queries.wait_recv()

    def token_of(index):
        slot = index // rows
        base = jnp.zeros_like(index)
        for number in range(4):
            base = jnp.where(slot == number, ((place + steps[number]) % 4) * rows, base)
        return base + index % rows

    key_token = token_of(lax.broadcasted_iota(jnp.int32, (1, tokens), 1))
    query_token = shard * tokens + token_of(lax.broadcasted_iota(jnp.int32, (tokens, 1), 0))

    def turn(step):
        if step == 1:
            climbed(0, 1)
        elif step == 2:
            climbed(2, 0)
            climbed(1, 1)
            pl.when(x > 0)(got_right)
            pl.when(x == 3)(got_left)
        elif step == 3:
            spread(1, 0)
            spread(0, 1)
        elif step == 5:
            climbed(3, 0)
            climbed(2, 1)
        elif step == 6:
            spread(2, 0)
            climbed(3, 1)
        elif step == 7:
            spread(1, 1)
        elif step == 9:
            passed(0)
        elif step == 10:
            spread(2, 1)
        elif step == 12:
            pl.when(x == 0)(got_right)
            pl.when(x < 3)(got_left)
        elif step == 14:
            passed(1)
        elif step == 15:
            passed(2)
        elif step == 16:
            for part in range(2):
                for kind in range(2):
                    edge_far(kind, part).wait_recv()

    def visit(step, carried):
        for number in (1, 2, 3, 5, 6, 7, 9, 10, 12, 14, 15, 16):
            pl.when(step == number)(functools.partial(turn, number))
        keys = meta[0, step] + key_token
        listed = meta[1, step] == 1
        start = jnp.where(listed, starts[:, :1], shard * tokens + tokens)
        seen = (keys >= start) & (keys <= query_token)
        wide[:, :HEAD_WIDTH] = blocks[step, :, HEAD_WIDTH:]
        for head in range(4):
            scores = lax.dot_general(
                queries[head],
                blocks[step, :, :HEAD_WIDTH],
                (((1,), (1,)), ((), ())),
                preferred_element_type=jnp.float32,
            )
            raised = jnp.where(seen, jnp.exp2(jnp.tanh(scores) * RAISE), 0.0)
            total[head] += jnp.dot(
                raised.astype(jnp.bfloat16), wide[...], preferred_element_type=jnp.float32
            )
        return carried

    lax.fori_loop(0, len(SLOTS), visit, 0)

    for mine in range(2):
        value = total[2 * other + mine]
        ready[:, mine * HEAD_WIDTH : (mine + 1) * HEAD_WIDTH] = (
            value[:, :HEAD_WIDTH] / value[:, HEAD_WIDTH:]
        ).astype(jnp.bfloat16)
    swap_back = start_copy(ready, heads.at[section], swap_s.at[1], swap_r.at[1], section=other)
    swap_back.start()
    for mine in range(2):
        value = total[2 * section + mine]
        heads[section, :, mine * HEAD_WIDTH : (mine + 1) * HEAD_WIDTH] = (
            value[:, :HEAD_WIDTH] / value[:, HEAD_WIDTH:]
        ).astype(jnp.bfloat16)
    fetch_out.wait()
    swap_back.wait_recv()

    near_slot = (2, 1)
    inner = 2 * HEAD_WIDTH

    def partial(slot, low):
        span = slice(slot * rows, (slot + 1) * rows)
        return jnp.dot(
            heads[0, span, :], out_weight[:inner, low : low + piece], preferred_element_type=jnp.float32
        ) + jnp.dot(
            heads[1, span, :], out_weight[inner:, low : low + piece], preferred_element_type=jnp.float32
        )

    def send(source, target, sent, landed, side, part):
        return start_copy(
            source.at[side, part], target.at[side, part], sent.at[side, part], landed.at[side, part],
            head=sides[side],
        )

    def far_copy(side, part):
        return send(far_out, far_in, far_s, far_r, side, part)

    def near_copy(side, part):
        return send(near_out, near_in, near_s, near_r, side, part)

    def sum_copy(side, part):
        return send(sum_out, sum_in, sum_s, sum_r, side, part)

    for part in range(PIECES):
        for side in range(2):
            far_out[side, part] = partial(3, side * half + part * piece).astype(jnp.bfloat16)
            far_copy(side, part).start()
    for part in range(PIECES):
        for side in range(2):
            low = (1 - side) * half + part * piece
            near_out[side, part] = partial(near_slot[side], low).astype(jnp.bfloat16)
            near_copy(side, part).start()
    for part in range(PIECES):
        for side in range(2):
            low = side * half + part * piece
            own = partial(near_slot[side], low).astype(jnp.bfloat16).astype(jnp.float32)
            far_copy(side, part).wait_recv()
            sum_out[side, part] = (own + far_in[side, part].astype(jnp.float32)).astype(jnp.bfloat16)
            sum_copy(side, part).start()
    for part in range(2 * PIECES):
        low = part * piece
        mixed[:, low : low + piece] = partial(0, low).astype(jnp.bfloat16).astype(jnp.float32)
    for part in range(PIECES):
        for side in range(2):
            low = (1 - side) * half + part * piece
            near_copy(side, part).wait_recv()
            mixed[:, low : low + piece] += near_in[side, part].astype(jnp.float32)
    squares = jnp.zeros((rows, 128), jnp.float32)
    for part in range(PIECES):
        for side in range(2):
            low = side * half + part * piece
            sum_copy(side, part).wait_recv()
            value = mixed[:, low : low + piece] + sum_in[side, part].astype(jnp.float32)
            mixed[:, low : low + piece] = value
            square = value * value
            for column in range(0, piece, 128):
                squares = squares + square[:, column : column + 128]
    scale = lax.rsqrt(jnp.sum(squares, axis=-1, keepdims=True) / width + epsilon)
    for part in range(2 * PIECES):
        span = slice(part * piece, (part + 1) * piece)
        out_ref[:, span] = (
            hidden_ref[:, span].astype(jnp.float32) + mixed[:, span] * scale * post_ref[:, span]
        ).astype(jnp.bfloat16)

    for side in range(2):
        for part in range(PIECES):
            for kind in range(3):
                row_copy(side, kind, part).wait_send()
            far_copy(side, part).wait_send()
            near_copy(side, part).wait_send()
            sum_copy(side, part).wait_send()
    swap_back.wait_send()
    swap_queries.wait_send()
    for part in range(2):
        for step in range(4):
            climb(step, part).wait_send()
        for row in range(3):
            to_right(row, part).wait_send()
            to_left(row, part).wait_send()
            pass_keys(row, part).wait_send()
            pass_values(row, part).wait_send()
        edge_right(0, part).wait_send()
        edge_left(0, part).wait_send()
        for kind in range(4):
            pl.when(far_when[kind])(edge_far(kind, part).wait_send)

    @pl.when(section == 0)
    def _():
        for part in range(2):
            hand_keys(part).wait_send()
        for number in range(3):
            share_across(number).wait_send()
        for at in climbs:
            climb_weights(*at).wait_send()


def layer(table, hidden, gain, cosine, sine, query_weight, share, starts, out_weight, post_gain):
    rows, width = hidden.shape
    tokens = starts.shape[0]
    dma = pltpu.SemaphoreType.DMA
    whole = pl.BlockSpec(memory_space=pltpu.VMEM)
    apart = pl.BlockSpec(memory_space=pl.ANY)
    small = pl.BlockSpec(memory_space=pltpu.SMEM)
    pieces = pltpu.VMEM((2, PIECES, rows, width // (2 * PIECES)), jnp.bfloat16)

    def half_type(*shape):
        return pltpu.VMEM(shape, jnp.bfloat16)

    pair = 2 * HEAD_WIDTH
    return pl.pallas_call(
        layer_kernel,
        out_shape=jax.ShapeDtypeStruct((rows, width), jnp.bfloat16),
        in_specs=[small, whole, whole, whole, whole, apart, whole, whole, apart, whole],
        out_specs=whole,
        scratch_shapes=[
            pltpu.SMEM((2, len(SLOTS)), jnp.int32),
            half_type(4, rows, width),
            half_type(*query_weight.shape),
            half_type(width, share.shape[1]),
            half_type(*out_weight.shape),
            half_type(4, tokens, HEAD_WIDTH),
            half_type(2, tokens, pair),
            half_type(4, tokens, HEAD_WIDTH),
            half_type(len(SLOTS), tokens, pair),
            pltpu.VMEM((tokens, HEAD_WIDTH), jnp.int32),
            pltpu.VMEM((4, tokens, pair), jnp.float32),
            half_type(tokens, pair),
            half_type(tokens, pair),
            half_type(2, tokens, pair),
            pieces, pieces, pieces, pieces, pieces, pieces,
            pltpu.VMEM((rows, width), jnp.float32),
            dma((2,)), dma((2, 3, PIECES)), dma((2, 3, PIECES)), dma((3,)), dma((3,)),
            dma((2, 4, 4)), dma((2, 4, 4)), dma((2,)), dma((2,)), dma((3,)), dma((2,)), dma((2,)),
            dma((4, 2)), dma((4, 2)), dma((4, 2)), dma((4, 2)), dma((4, 2)), dma((4, 2)),
            dma((3, 2)), dma((3, 2)), dma((3, 2)), dma((3, 2)), dma((4, 2)), dma((2, 2)),
        ]
        + [dma((2, PIECES))] * 6,
        compiler_params=pltpu.CompilerParams(
            collective_id=1, has_side_effects=True, vmem_limit_bytes=62 * 2**20
        ),
        name="layer",
    )(table, hidden, gain, cosine, sine, query_weight, share, starts, out_weight, post_gain)


def local(hidden, q_weight, key_value_weight, o_weight, in_gain, post_gain, positions, block_table):
    shard = lax.axis_index("seq")
    tokens = 4 * hidden.shape[1]
    first = shard * tokens
    at = lax.dynamic_slice_in_dim(positions, first, tokens)
    lane = jnp.arange(HEAD_WIDTH, dtype=jnp.int32)
    frequency = 10000.0 ** (-((lane % (HEAD_WIDTH // 2)).astype(jnp.float32) * 2.0 / HEAD_WIDTH))
    angles = at.astype(jnp.float32)[:, None] * frequency[None, :]
    sine = jnp.sin(angles) * jnp.where(lane < HEAD_WIDTH // 2, -1.0, 1.0)
    share = key_value_weight.reshape(key_value_weight.shape[0], -1)
    starts = jnp.broadcast_to(
        (first + jnp.arange(tokens, dtype=jnp.int32) - at)[:, None], (tokens, HEAD_WIDTH)
    )
    return layer(
        block_table, hidden[0], in_gain, jnp.cos(angles), sine, q_weight[0], share, starts, o_weight[0], post_gain
    )[None]


def solution(mesh):
    placed = (
        P("section", ("seq", "head"), None),
        P("section", None, "head"),
        P("seq", None, "head"),
        P("section", "head", None),
        P("section", None),
        P("section", None),
        P(),
        P(),
    )
    return jax.shard_map(
        local,
        mesh=mesh,
        in_specs=placed,
        out_specs=P("section", ("seq", "head"), None),
        check_vma=False,
    )
```

time: 289 us -> 147 us (0.51)
  waiting for transfers between devices: 122 us -> 0 us
  Pallas kernels: 119 us -> 138 us
  between operations: 13.6 us -> 0.01 us
  matrix products: 12 us -> 0 us
  local copies, waits for them, and re-layouts: 13.3 us -> 4.79 us
  other arithmetic: 8.76 us -> 2.58 us
    all_gather x2 -> x0, waiting for transfers between devices: 121 us -> none  [the longest x1 72.3 us: local(): lax.all_gather(key_value_weight, 'seq', axis=0, tiled=True)]
    pallas_call x2 -> x1, Pallas kernels: 119 us -> 138 us  [layer(): pl.pallas_call(layer_kernel, out_shape=jax.ShapeDtypeStruct((rows, width)...]
    dot_general x2 -> x0, matrix products: 12 us -> none  [the longest x1 7.23 us: local(): jnp.einsum('td,dce->tce', normed, lax.all_gather(key_value_weight, 'seq',...]
    dot_general x2 -> x0, local copies, waits for them, and re-layouts: 6.99 us -> none  [the longest x1 6.78 us: local(): jnp.dot(normed, q_weight[0], preferred_element_type=jnp.float32)]
    reduce_sum x1 -> x0, other arithmetic: 3.48 us -> none  [normalize(): jnp.mean(values * values, axis=-1, keepdims=True) + epsilon]
  transfers between devices with their start and end apart: 2 -> 0, of which waited for: 2 -> 0; matrix products, arithmetic and copies ran while one was open for 7% -> 0% of each run, Pallas kernels for 0% -> 0%
where the time goes in v4:
time: 147 us; the launch traced here: 145 us
  Pallas kernels  138 us (94%)
  local copies, waits for them, and re-layouts  4.79 us (3%)
  other arithmetic  2.58 us (2%)
    pallas_call x1, Pallas kernels, layer(): pl.pallas_call(layer_kernel, out_shape=jax.ShapeDtypeStruct((rows, width)...  138 us
    unnamed x2, local copies, waits for them, and re-layouts  3.95 us

profile of v4, /device:TPU:1, one launch (start us, length us, event | category | flops | bytes accessed | tf_op | source)
XLA Modules:
  0.0 145.2 jit_solution(9019957037921860516)
XLA Ops:
  0.0 0.8 add_subtract_fusion
  0.8 1.6 %copy.9 = bf16[18,8,2,256]{3,1,2,0:T(8,128)(2,1)} copy(bf16[18,8,2,256]{3,2,1,0:T(2,128)(2,1)} %bitcast.11) | data formatting | bytes 294912
  2.4 0.8 broadcast_in_dim.22.start_ref
  3.2 1.8 %fusion = (f32[512,128]{1,0:T(8,128)}, f32[512,128]{1,0:T(8,128)}) fusion(f32[128]{0:T(128)S(1)} %get-tuple-element.9, f32[128]{0:T(128)S(1)} %get-tuple-element.10, f32[512]{0:T(512)S(1)} %get-tuple-element.6), kind=kLoop, calls=%fused_computation.2 | loop fusion | flops 131072 | bytes 527360 | tf_op jit(solution)/shard_map/mul | solution.py:595
  5.0 137.8 %layer.1 = bf16[128,4608]{1,0:T(8,128)(2,1)} custom-call(s32[32,32]{1,0:T(8,128)} %table.1, bf16[128,4608]{1,0:T(8,128)(2,1)} %bitcast.9, f32[1,4608]{1,0:T(1,128)} %gain_ref.1, f32[512,128]{1,0:T(8,128)} %get-tuple-element.8.cos_ref, f32[512,128]{1,0:T(8,128)} %get-tuple-element.7.sin_ref, bf16[4608,512]{1,0:T(8,128)(2,1)} %bitcast.7, ...), custom_call_target="tpu_custom_call" | custom-call | tf_op jit(solution)/shard_map/layer/pallas_call | solution.py:552
  142.8 2.4 %copy.11 = bf16[1,128,4608]{2,1,0:T(8,128)(2,1)} copy(bf16[1,128,4608]{2,1,0:T(8,128)(2,1)} %bitcast.6) | data formatting | bytes 2359296
  (1 shorter events, 0.0 us)

commit v5 on v4

--- a/solution.py
+++ b/solution.py
@@ -23,7 +23,9 @@
     (0, 0), (1, 0), (2, 0), (1, 1), (1, 3), (3, 0), (4, 0), (2, 1), (2, 3),
     (1, 2), (3, 1), (3, 3), (-1, 1), (-1, 3), (2, 2), (3, 2), (-1, 2),
 )
-PARTS = ((0, 384), (384, 128))
+PARTS = ((0, 128), (128, 256), (384, 128))
+BACK = ((384, 128), (0, 384))
+FIRST = 64
 PIECES = 3
 
 
@@ -49,10 +51,10 @@
 
 
 def layer_kernel(
-    table, hidden_ref, gain_ref, cos_ref, sin_ref, query_hbm, share_ref, start_ref, out_hbm, post_ref, out_ref,
-    meta, normed, query_weight, kv_weight, out_weight, made_queries, made_kv, queries, blocks, starts,
+    table, hidden_ref, gain_ref, position_ref, frequency_ref, query_hbm, share_ref, out_hbm, post_ref, out_ref,
+    meta, normed, query_weight, kv_weight, out_weight, made_queries, made_kv, queries, blocks, starts, cosine, sine,
     total, wide, ready, heads, far_out, near_out, sum_out, far_in, near_in, sum_in, mixed,
-    load, side_s, side_r, x_s, x_r, w_s, w_r, swap_s, swap_r, own_s, hand_s, hand_r,
+    load, side_s, side_r, x_s, x_r, w_s, w_r, b_s, b_r, c_s, c_r, d_s, d_r, swap_s, swap_r, own_s, hand_s, hand_r,
     z_s, z_r, right_s, right_r, left_s, left_r, key_s, key_r, value_s, value_r, edge_s, edge_r,
     far_s, far_r, near_s, near_r, sum_s, sum_r,
 ):
@@ -66,7 +68,7 @@
     across = [z * XS + (x + step) % XS for step in (1, 3, 2)]
     right, left = across[0], across[1]
     rows, width = hidden_ref.shape
-    tokens = start_ref.shape[0]
+    tokens = 4 * rows
     half = width // 2
     piece = half // PIECES
     depth = share_ref.shape[0]
@@ -75,27 +77,30 @@
     fetch = pltpu.make_async_copy(query_hbm, query_weight, load.at[0])
     fetch.start()
     fetch_out = pltpu.make_async_copy(out_hbm, out_weight, load.at[1])
+    own_share = pl.ds(pl.multiple_of(shard * depth, 16), depth)
+    columns = share_ref.shape[2]
+    for number in range(2):
+        kv_weight[own_share, number * columns : (number + 1) * columns] = share_ref[:, number, :]
     greet(
         [{"head": sides[0]}, {"head": sides[1]}, {"section": other}]
         + [{"seq": seq} for seq in across + [up, down]]
     )
 
-    def weight_rows(zz, xx):
-        return pl.ds(pl.multiple_of((zz * XS + xx) * depth, 16), depth)
+    def weight_rows(zz, xx, second):
+        low = (zz * XS + xx) * depth + (FIRST if second else 0)
+        return pl.ds(pl.multiple_of(low, 16), depth - FIRST if second else FIRST)
+
+    def weight_copy(zz, xx, second, sent, landed, seq):
+        span = weight_rows(zz % ZS, xx % XS, second)
+        return start_copy(kv_weight.at[span], kv_weight.at[span], sent, landed, seq=seq)
 
     def share_across(number):
-        return start_copy(
-            share_ref, kv_weight.at[weight_rows(z, x)], x_s.at[number], x_r.at[number], seq=across[number]
-        )
+        return weight_copy(z, x, False, x_s.at[number], x_r.at[number], across[number])
 
     def climb_weights(side, hop, aside):
-        back = hop - 1
-        origin = (z + ZS - back) % ZS if side == 0 else (z + back) % ZS
-        span = weight_rows(origin, (x + aside) % XS)
-        source = share_ref if hop == 1 and aside == 0 else kv_weight.at[span]
-        return start_copy(
-            source, kv_weight.at[span], w_s.at[side, hop - 1, aside], w_r.at[side, hop - 1, aside],
-            seq=(up, down)[side],
+        origin = z + ZS - (hop - 1) if side == 0 else z + (hop - 1)
+        return weight_copy(
+            origin, x + aside, False, w_s.at[side, hop - 1, aside], w_r.at[side, hop - 1, aside], (up, down)[side]
         )
 
     climbs = [
@@ -105,6 +110,23 @@
         for side in range(2)
         if hop < 4 or (aside < 2) == (side == 0)
     ]
+
+    def climb_second(side, hop):
+        origin = z + ZS - (hop - 1) if side == 0 else z + (hop - 1)
+        return weight_copy(origin, x, True, b_s.at[side, hop - 1], b_r.at[side, hop - 1], (up, down)[side])
+
+    second_climbs = [(side, hop) for hop in range(1, 5) for side in range(2) if hop < 4 or side == 0]
+
+    def cross_second(side, back):
+        return weight_copy(
+            z + ZS - back, x, True, c_s.at[side, back], c_r.at[side, back], (right, left)[side]
+        )
+
+    def relay_second(back):
+        side = back % 2
+        return weight_copy(
+            z + ZS - back, x + (3, 1)[side], True, d_s.at[back], d_r.at[back], (right, left)[side]
+        )
 
     def row_copy(side, kind, part):
         which = side if kind == 0 else 1 - side
@@ -116,16 +138,14 @@
             side_s.at[side, kind, part], side_r.at[side, kind, part], head=sides[side],
         )
 
-    def token_rows(slot):
-        return pl.ds(pl.multiple_of(((place + steps[slot]) % 4) * rows, rows), rows)
-
     @pl.when(section == 0)
     def _():
         for number in range(3):
             share_across(number).start()
         for side in range(2):
+            climb_second(side, 1).start()
             climb_weights(side, 1, 0).start()
-        kv_weight[weight_rows(z, x), :] = share_ref[...]
+            cross_second(side, 0).start()
 
     squares = jnp.zeros((rows, 128), jnp.float32)
     for column in range(0, width, 128):
@@ -155,8 +175,16 @@
         block = (z - row) * XS + source
         meta[0, number] = block * tokens
         meta[1, number] = table[shard, jnp.maximum(block, 0)]
+    lane = lax.broadcasted_iota(jnp.int32, (rows, HEAD_WIDTH), 1)
+    line = lax.broadcasted_iota(jnp.int32, (rows, HEAD_WIDTH), 0)
     for slot in range(4):
-        starts[slot * rows : (slot + 1) * rows, :] = start_ref[token_rows(slot), :]
+        origin = (place + steps[slot]) % 4
+        span = slice(slot * rows, (slot + 1) * rows)
+        at = jnp.transpose(jnp.broadcast_to(position_ref[pl.ds(4 * shard + origin, 1), :], (rows, rows)))
+        starts[span, :] = shard * tokens + origin * rows + line - at
+        angle = at.astype(jnp.float32) * frequency_ref[...]
+        cosine[span, :] = jnp.cos(angle)
+        sine[span, :] = jnp.sin(angle) * jnp.where(lane < HEAD_WIDTH // 2, -1.0, 1.0)
     total[...] = jnp.zeros_like(total)
     wide[...] = jnp.ones_like(wide)
 
@@ -168,7 +196,7 @@
         )
 
     def turned(value, span):
-        return value * cos_ref[span, :] + pltpu.roll(value, HEAD_WIDTH // 2, 1) * sin_ref[span, :]
+        return value * cosine[span, :] + pltpu.roll(value, HEAD_WIDTH // 2, 1) * sine[span, :]
 
     def make_queries(first, count):
         for pair in range(2):
@@ -178,7 +206,7 @@
                 for mine in range(2):
                     value = result[slot * rows : (slot + 1) * rows, mine * HEAD_WIDTH : (mine + 1) * HEAD_WIDTH]
                     made_queries[2 * pair + mine, low : low + rows, :] = (
-                        turned(value, token_rows(first + slot)) * (query_scale / softcap_limit)
+                        turned(value, slice(low, low + rows)) * (query_scale / softcap_limit)
                     ).astype(jnp.bfloat16)
 
     def make_keys(first, count):
@@ -189,7 +217,7 @@
                 for mine in range(2):
                     value = result[slot * rows : (slot + 1) * rows, mine * HEAD_WIDTH : (mine + 1) * HEAD_WIDTH]
                     if pair == 0:
-                        value = turned(value, token_rows(first + slot))
+                        value = turned(value, slice(low, low + rows))
                     made_kv[mine, low : low + rows, pair * HEAD_WIDTH : (pair + 1) * HEAD_WIDTH] = value.astype(
                         jnp.bfloat16
                     )
@@ -197,11 +225,29 @@
     def pass_weights(hop):
         @pl.when(section == 0)
         def _():
+            for side, at in second_climbs:
+                if at == hop:
+                    climb_second(side, hop).wait_recv()
+                    if (side, hop + 1) in second_climbs:
+                        climb_second(side, hop + 1).start()
+                    for across_side in range(2):
+                        cross_second(across_side, hop if side == 0 else ZS - hop).start()
             for side, at, aside in climbs:
                 if at == hop:
                     climb_weights(side, hop, aside).wait_recv()
                     if (side, hop + 1, aside) in climbs:
                         climb_weights(side, hop + 1, aside).start()
+            for back in ((0,), (1, 7), (2, 6), (3, 5), (4,))[hop - 1]:
+                for side in range(2):
+                    cross_second(side, back).wait_recv()
+                relay_second(back).start()
+
+    def finish_weights():
+        for side in range(2):
+            cross_second(side, 4).wait_recv()
+        relay_second(4).start()
+        for back in range(ZS):
+            relay_second(back).wait_recv()
 
     def span_of(part):
         return pl.ds(*PARTS[part])
@@ -280,21 +326,34 @@
         pass_values(row, part).start()
 
     def passed(row):
-        for part in range(2):
+        for part in range(3):
             pass_keys(row, part).wait_recv()
             pass_values(row, part).wait_recv()
 
-    def got_right():
-        for part in range(2):
-            edge_right(0, part).wait_recv()
-            for kind in (0, 1):
-                pl.when(far_when[kind])(edge_far(kind, part).start)
-
-    def got_left():
-        for part in range(2):
-            edge_left(0, part).wait_recv()
-            for kind in (2, 3):
-                pl.when(far_when[kind])(edge_far(kind, part).start)
+    def got_right(part):
+        edge_right(0, part).wait_recv()
+        for kind in (0, 1):
+            pl.when(far_when[kind])(edge_far(kind, part).start)
+
+    def got_left(part):
+        edge_left(0, part).wait_recv()
+        for kind in (2, 3):
+            pl.when(far_when[kind])(edge_far(kind, part).start)
+
+    def late_edge(part):
+        pl.when(x == 0)(lambda: got_right(part))
+        pl.when(x < 3)(lambda: got_left(part))
+
+    def give_keys(part, first, count):
+        @pl.when(section == 0)
+        def _():
+            make_keys(first, count)
+            hand_keys(part).start()
+            own_keys(part).start()
+            own_keys(part).wait()
+
+        pl.when(section == 1)(lambda: hand_keys(part).wait_recv())
+        begin(part)
 
     fetch.wait()
     make_queries(0, 1)
@@ -305,40 +364,28 @@
             row_copy(side, 0, part).wait_recv()
             row_copy(side, 2, part).start()
     pass_weights(3)
+    pass_weights(4)
+    pl.when(section == 0)(finish_weights)
+    give_keys(0, 0, 1)
     for part in range(PIECES):
         for side in range(2):
             row_copy(side, 1, part).wait_recv()
-    pass_weights(4)
-
-    @pl.when(section == 0)
-    def _():
-        make_keys(0, 3)
-        hand_keys(0).start()
-        own_keys(0).start()
-        own_keys(0).wait()
-
-    @pl.when(section == 1)
-    def _():
-        make_queries(1, 2)
-        hand_keys(0).wait_recv()
-
-    begin(0)
+    pl.when(section == 1)(lambda: make_queries(1, 2))
+    give_keys(1, 1, 2)
+    climbed(0, 0)
     pl.when(section == 0)(lambda: make_queries(1, 2))
     fetch_out.start()
-    climbed(0, 0)
+    spread(0, 0)
+    climbed(1, 0)
+    climbed(0, 1)
+    climbed(2, 0)
+    spread(1, 0)
     for part in range(PIECES):
         for side in range(2):
             row_copy(side, 2, part).wait_recv()
-
-    @pl.when(section == 0)
-    def _():
-        make_keys(3, 1)
-        hand_keys(1).start()
-        own_keys(1).start()
-        own_keys(1).wait()
-
-    pl.when(section == 1)(lambda: hand_keys(1).wait_recv())
-    begin(1)
+    give_keys(2, 3, 1)
+    spread(0, 1)
+    climbed(1, 1)
     make_queries(3, 1)
     swap_queries = start_copy(
         made_queries.at[pl.ds(2 * other, 2)], queries.at[pl.ds(2 * section, 2)],
@@ -349,8 +396,7 @@
     )
     swap_queries.start()
     own_queries.start()
-    spread(0, 0)
-    climbed(1, 0)
+    climbed(3, 0)
     own_queries.wait()
     swap_queries.wait_recv()
 
@@ -366,36 +412,39 @@
 
     def turn(step):
         if step == 1:
-            climbed(0, 1)
+            climbed(0, 2)
+            climbed(2, 1)
         elif step == 2:
-            climbed(2, 0)
-            climbed(1, 1)
-            pl.when(x > 0)(got_right)
-            pl.when(x == 3)(got_left)
+            spread(2, 0)
+            climbed(1, 2)
+            for part in range(3):
+                pl.when(x > 0)(functools.partial(got_right, part))
+                pl.when(x == 3)(functools.partial(got_left, part))
         elif step == 3:
-            spread(1, 0)
-            spread(0, 1)
+            spread(1, 1)
+            spread(0, 2)
         elif step == 5:
-            climbed(3, 0)
-            climbed(2, 1)
+            climbed(3, 1)
+            climbed(2, 2)
         elif step == 6:
-            spread(2, 0)
-            climbed(3, 1)
+            spread(2, 1)
+            climbed(3, 2)
         elif step == 7:
-            spread(1, 1)
+            spread(1, 2)
+            late_edge(0)
         elif step == 9:
             passed(0)
         elif step == 10:
-            spread(2, 1)
+            spread(2, 2)
+            late_edge(1)
         elif step == 12:
-            pl.when(x == 0)(got_right)
-            pl.when(x < 3)(got_left)
+            late_edge(2)
         elif step == 14:
             passed(1)
         elif step == 15:
             passed(2)
         elif step == 16:
-            for part in range(2):
+            for part in range(3):
                 for kind in range(2):
                     edge_far(kind, part).wait_recv()
 
@@ -422,20 +471,29 @@
 
     lax.fori_loop(0, len(SLOTS), visit, 0)
 
-    for mine in range(2):
-        value = total[2 * other + mine]
-        ready[:, mine * HEAD_WIDTH : (mine + 1) * HEAD_WIDTH] = (
-            value[:, :HEAD_WIDTH] / value[:, HEAD_WIDTH:]
-        ).astype(jnp.bfloat16)
-    swap_back = start_copy(ready, heads.at[section], swap_s.at[1], swap_r.at[1], section=other)
-    swap_back.start()
-    for mine in range(2):
-        value = total[2 * section + mine]
-        heads[section, :, mine * HEAD_WIDTH : (mine + 1) * HEAD_WIDTH] = (
-            value[:, :HEAD_WIDTH] / value[:, HEAD_WIDTH:]
-        ).astype(jnp.bfloat16)
+    def swap_back(part):
+        span = pl.ds(*BACK[part])
+        return start_copy(
+            ready.at[span], heads.at[section, span], swap_s.at[1 + part], swap_r.at[1 + part], section=other
+        )
+
+    def share_of(owner, low, count, mine):
+        value = total[2 * owner + mine, low : low + count, :]
+        return (value[:, :HEAD_WIDTH] / value[:, HEAD_WIDTH:]).astype(jnp.bfloat16)
+
+    for part in range(2):
+        low, count = BACK[part]
+        for mine in range(2):
+            lanes = slice(mine * HEAD_WIDTH, (mine + 1) * HEAD_WIDTH)
+            ready[low : low + count, lanes] = share_of(other, low, count, mine)
+        swap_back(part).start()
+    for part in range(2):
+        low, count = BACK[part]
+        for mine in range(2):
+            lanes = slice(mine * HEAD_WIDTH, (mine + 1) * HEAD_WIDTH)
+            heads[section, low : low + count, lanes] = share_of(section, low, count, mine)
     fetch_out.wait()
-    swap_back.wait_recv()
+    swap_back(0).wait_recv()
 
     near_slot = (2, 1)
     inner = 2 * HEAD_WIDTH
@@ -467,6 +525,7 @@
         for side in range(2):
             far_out[side, part] = partial(3, side * half + part * piece).astype(jnp.bfloat16)
             far_copy(side, part).start()
+    swap_back(1).wait_recv()
     for part in range(PIECES):
         for side in range(2):
             low = (1 - side) * half + part * piece
@@ -511,9 +570,10 @@
             far_copy(side, part).wait_send()
             near_copy(side, part).wait_send()
             sum_copy(side, part).wait_send()
-    swap_back.wait_send()
+    for part in range(2):
+        swap_back(part).wait_send()
     swap_queries.wait_send()
-    for part in range(2):
+    for part in range(3):
         for step in range(4):
             climb(step, part).wait_send()
         for row in range(3):
@@ -528,17 +588,23 @@
 
     @pl.when(section == 0)
     def _():
-        for part in range(2):
+        for part in range(3):
             hand_keys(part).wait_send()
         for number in range(3):
             share_across(number).wait_send()
         for at in climbs:
             climb_weights(*at).wait_send()
-
-
-def layer(table, hidden, gain, cosine, sine, query_weight, share, starts, out_weight, post_gain):
+        for at in second_climbs:
+            climb_second(*at).wait_send()
+        for back in range(ZS):
+            for side in range(2):
+                cross_second(side, back).wait_send()
+            relay_second(back).wait_send()
+
+
+def layer(table, hidden, gain, positions, frequency, query_weight, share, out_weight, post_gain):
     rows, width = hidden.shape
-    tokens = starts.shape[0]
+    tokens = 4 * rows
     dma = pltpu.SemaphoreType.DMA
     whole = pl.BlockSpec(memory_space=pltpu.VMEM)
     apart = pl.BlockSpec(memory_space=pl.ANY)
@@ -552,19 +618,21 @@
     return pl.pallas_call(
         layer_kernel,
         out_shape=jax.ShapeDtypeStruct((rows, width), jnp.bfloat16),
-        in_specs=[small, whole, whole, whole, whole, apart, whole, whole, apart, whole],
+        in_specs=[small, whole, whole, whole, whole, apart, whole, apart, whole],
         out_specs=whole,
         scratch_shapes=[
             pltpu.SMEM((2, len(SLOTS)), jnp.int32),
             half_type(4, rows, width),
             half_type(*query_weight.shape),
-            half_type(width, share.shape[1]),
+            half_type(width, share.shape[1] * share.shape[2]),
             half_type(*out_weight.shape),
             half_type(4, tokens, HEAD_WIDTH),
             half_type(2, tokens, pair),
             half_type(4, tokens, HEAD_WIDTH),
             half_type(len(SLOTS), tokens, pair),
             pltpu.VMEM((tokens, HEAD_WIDTH), jnp.int32),
+            pltpu.VMEM((tokens, HEAD_WIDTH), jnp.float32),
+            pltpu.VMEM((tokens, HEAD_WIDTH), jnp.float32),
             pltpu.VMEM((4, tokens, pair), jnp.float32),
             half_type(tokens, pair),
             half_type(tokens, pair),
@@ -572,33 +640,25 @@
             pieces, pieces, pieces, pieces, pieces, pieces,
             pltpu.VMEM((rows, width), jnp.float32),
             dma((2,)), dma((2, 3, PIECES)), dma((2, 3, PIECES)), dma((3,)), dma((3,)),
-            dma((2, 4, 4)), dma((2, 4, 4)), dma((2,)), dma((2,)), dma((3,)), dma((2,)), dma((2,)),
-            dma((4, 2)), dma((4, 2)), dma((4, 2)), dma((4, 2)), dma((4, 2)), dma((4, 2)),
-            dma((3, 2)), dma((3, 2)), dma((3, 2)), dma((3, 2)), dma((4, 2)), dma((2, 2)),
+            dma((2, 4, 4)), dma((2, 4, 4)), dma((2, 4)), dma((2, 4)), dma((2, ZS)), dma((2, ZS)), dma((ZS,)), dma((ZS,)),
+            dma((3,)), dma((3,)), dma((4,)), dma((3,)), dma((3,)),
+            dma((4, 3)), dma((4, 3)), dma((4, 3)), dma((4, 3)), dma((4, 3)), dma((4, 3)),
+            dma((3, 3)), dma((3, 3)), dma((3, 3)), dma((3, 3)), dma((4, 3)), dma((2, 3)),
         ]
         + [dma((2, PIECES))] * 6,
         compiler_params=pltpu.CompilerParams(
             collective_id=1, has_side_effects=True, vmem_limit_bytes=62 * 2**20
         ),
         name="layer",
-    )(table, hidden, gain, cosine, sine, query_weight, share, starts, out_weight, post_gain)
+    )(table, hidden, gain, positions, frequency, query_weight, share, out_weight, post_gain)
 
 
 def local(hidden, q_weight, key_value_weight, o_weight, in_gain, post_gain, positions, block_table):
-    shard = lax.axis_index("seq")
-    tokens = 4 * hidden.shape[1]
-    first = shard * tokens
-    at = lax.dynamic_slice_in_dim(positions, first, tokens)
-    lane = jnp.arange(HEAD_WIDTH, dtype=jnp.int32)
-    frequency = 10000.0 ** (-((lane % (HEAD_WIDTH // 2)).astype(jnp.float32) * 2.0 / HEAD_WIDTH))
-    angles = at.astype(jnp.float32)[:, None] * frequency[None, :]
-    sine = jnp.sin(angles) * jnp.where(lane < HEAD_WIDTH // 2, -1.0, 1.0)
-    share = key_value_weight.reshape(key_value_weight.shape[0], -1)
-    starts = jnp.broadcast_to(
-        (first + jnp.arange(tokens, dtype=jnp.int32) - at)[:, None], (tokens, HEAD_WIDTH)
-    )
+    lane = jnp.arange(HEAD_WIDTH, dtype=jnp.int32) % (HEAD_WIDTH // 2)
+    frequency = 10000.0 ** (-(lane.astype(jnp.float32) * 2.0 / HEAD_WIDTH))
     return layer(
-        block_table, hidden[0], in_gain, jnp.cos(angles), sine, q_weight[0], share, starts, o_weight[0], post_gain
+        block_table, hidden[0], in_gain, positions.reshape(-1, hidden.shape[1]), frequency[None],
+        q_weight[0], key_value_weight, o_weight[0], post_gain,
     )[None]
 
 

time: 147 us -> 139 us (0.946); the launches traced: 145 us -> 139 us
  local copies, waits for them, and re-layouts: 4.79 us -> 2.36 us
  other arithmetic: 2.58 us -> 0.52 us
  Pallas kernels: 138 us -> 136 us
    pallas_call x1, Pallas kernels: 138 us -> 136 us  [layer(): pl.pallas_call(layer_kernel, out_shape=jax.ShapeDtypeStruct((rows, width)...]
    mul x1 -> x0, other arithmetic: 1.8 us -> none  [local(): sine = jnp.sin(angles) * jnp.where(lane < HEAD_WIDTH // 2, -1.0, 1.0)]
    unnamed x2 -> x1, local copies, waits for them, and re-layouts: 3.95 us -> 2.36 us
where the time goes in v5:
time: 139 us
  Pallas kernels  136 us (98%)
  local copies, waits for them, and re-layouts  2.36 us (2%)
    pallas_call x1, Pallas kernels, layer(): pl.pallas_call(layer_kernel, out_shape=jax.ShapeDtypeStruct((rows, width)...  136 us

profile of v5, /device:TPU:1, one launch (start us, length us, event | category | flops | bytes accessed | tf_op | source)
XLA Modules:
  0.0 138.8 jit_solution(17273210294846706457)
XLA Ops:
  0.0 0.5 fusion.3.frequency_ref
  0.5 135.9 %layer.1 = bf16[128,4608]{1,0:T(8,128)(2,1)} custom-call(s32[32,32]{1,0:T(8,128)} %table.1, bf16[128,4608]{1,0:T(8,128)(2,1)} %bitcast.8, f32[1,4608]{1,0:T(1,128)} %gain_ref.1, s32[128,128]{1,0:T(8,128)} %bitcast.9, f32[1,128]{1,0:T(1,128)} %fusion.3.frequency_ref, bf16[4608,512]{1,0:T(8,128)(2,1)} %bitcast.6, bf16[144,2,256]{2,1,0:T(2,128)(2,1)} %share_ref.1, ...), custom_call_target="tpu_custom_call" | custom-call | tf_op jit(solution)/shard_map/layer/pallas_call | solution.py:618
  136.4 2.4 %copy.10 = bf16[1,128,4608]{2,1,0:T(8,128)(2,1)} copy(bf16[1,128,4608]{2,1,0:T(8,128)(2,1)} %bitcast.5) | data formatting | bytes 2359296

commit v6 on v5

--- a/solution.py
+++ b/solution.py
@@ -4,6 +4,7 @@
 
 import jax
 import jax.numpy as jnp
+import numpy as np
 from jax import lax
 from jax.experimental import pallas as pl
 from jax.experimental.pallas import tpu as pltpu
@@ -175,19 +176,6 @@
         block = (z - row) * XS + source
         meta[0, number] = block * tokens
         meta[1, number] = table[shard, jnp.maximum(block, 0)]
-    lane = lax.broadcasted_iota(jnp.int32, (rows, HEAD_WIDTH), 1)
-    line = lax.broadcasted_iota(jnp.int32, (rows, HEAD_WIDTH), 0)
-    for slot in range(4):
-        origin = (place + steps[slot]) % 4
-        span = slice(slot * rows, (slot + 1) * rows)
-        at = jnp.transpose(jnp.broadcast_to(position_ref[pl.ds(4 * shard + origin, 1), :], (rows, rows)))
-        starts[span, :] = shard * tokens + origin * rows + line - at
-        angle = at.astype(jnp.float32) * frequency_ref[...]
-        cosine[span, :] = jnp.cos(angle)
-        sine[span, :] = jnp.sin(angle) * jnp.where(lane < HEAD_WIDTH // 2, -1.0, 1.0)
-    total[...] = jnp.zeros_like(total)
-    wide[...] = jnp.ones_like(wide)
-
     def product(first, count, weight, low):
         return jnp.dot(
             normed[first : first + count].reshape(count * rows, width),
@@ -355,30 +343,43 @@
         pl.when(section == 1)(lambda: hand_keys(part).wait_recv())
         begin(part)
 
-    fetch.wait()
-    make_queries(0, 1)
     pass_weights(1)
     pass_weights(2)
+    lane = lax.broadcasted_iota(jnp.int32, (rows, HEAD_WIDTH), 1)
+    line = lax.broadcasted_iota(jnp.int32, (rows, HEAD_WIDTH), 0)
+    for slot in range(4):
+        origin = (place + steps[slot]) % 4
+        span = slice(slot * rows, (slot + 1) * rows)
+        at = jnp.transpose(jnp.broadcast_to(position_ref[pl.ds(4 * shard + origin, 1), :], (rows, rows)))
+        starts[span, :] = shard * tokens + origin * rows + line - at
+        angle = at.astype(jnp.float32) * frequency_ref[...]
+        cosine[span, :] = jnp.cos(angle)
+        sine[span, :] = jnp.sin(angle) * jnp.where(lane < HEAD_WIDTH // 2, -1.0, 1.0)
+    pass_weights(3)
     for part in range(PIECES):
         for side in range(2):
             row_copy(side, 0, part).wait_recv()
             row_copy(side, 2, part).start()
-    pass_weights(3)
     pass_weights(4)
     pl.when(section == 0)(finish_weights)
     give_keys(0, 0, 1)
+    fetch.wait()
+    make_queries(0, 1)
+    total[...] = jnp.zeros_like(total)
+    wide[...] = jnp.ones_like(wide)
+
     for part in range(PIECES):
         for side in range(2):
             row_copy(side, 1, part).wait_recv()
+    climbed(0, 0)
     pl.when(section == 1)(lambda: make_queries(1, 2))
     give_keys(1, 1, 2)
-    climbed(0, 0)
-    pl.when(section == 0)(lambda: make_queries(1, 2))
-    fetch_out.start()
     spread(0, 0)
     climbed(1, 0)
+    fetch_out.start()
+    pl.when(section == 0)(lambda: make_queries(1, 2))
+    climbed(2, 0)
     climbed(0, 1)
-    climbed(2, 0)
     spread(1, 0)
     for part in range(PIECES):
         for side in range(2):
@@ -654,8 +655,8 @@
 
 
 def local(hidden, q_weight, key_value_weight, o_weight, in_gain, post_gain, positions, block_table):
-    lane = jnp.arange(HEAD_WIDTH, dtype=jnp.int32) % (HEAD_WIDTH // 2)
-    frequency = 10000.0 ** (-(lane.astype(jnp.float32) * 2.0 / HEAD_WIDTH))
+    lane = np.arange(HEAD_WIDTH) % (HEAD_WIDTH // 2)
+    frequency = jnp.asarray((10000.0 ** (-lane * 2.0 / HEAD_WIDTH)).astype(np.float32))
     return layer(
         block_table, hidden[0], in_gain, positions.reshape(-1, hidden.shape[1]), frequency[None],
         q_weight[0], key_value_weight, o_weight[0], post_gain,

time: 139 us -> 139 us (level)
  no operation moved by 1% of the time
where the time goes in v6:
time: 139 us; the launch traced here: 138 us
  Pallas kernels  136 us (98%)
  local copies, waits for them, and re-layouts  2.36 us (2%)
    pallas_call x1, Pallas kernels, layer(): pl.pallas_call(layer_kernel, out_shape=jax.ShapeDtypeStruct((rows, width)...  136 us

profile of v6, /device:TPU:1, one launch (start us, length us, event | category | flops | bytes accessed | tf_op | source)
XLA Modules:
  0.0 138.4 jit_solution(11658547237804933115)
XLA Ops:
  0.0 136.1 %layer.1 = bf16[128,4608]{1,0:T(8,128)(2,1)} custom-call(s32[32,32]{1,0:T(8,128)} %table.1, bf16[128,4608]{1,0:T(8,128)(2,1)} %bitcast.8, f32[1,4608]{1,0:T(1,128)} %gain_ref.1, s32[128,128]{1,0:T(8,128)} %bitcast.9, f32[1,128]{1,0:T(1,128)} %constant.9.frequency_ref, bf16[4608,512]{1,0:T(8,128)(2,1)} %bitcast.6, bf16[144,2,256]{2,1,0:T(2,128)(2,1)} %share_ref.1, ...), custom_call_target="tpu_custom_call" | custom-call | tf_op jit(solution)/shard_map/layer/pallas_call | solution.py:619
  136.1 2.4 %copy.11 = bf16[1,128,4608]{2,1,0:T(8,128)(2,1)} copy(bf16[1,128,4608]{2,1,0:T(8,128)(2,1)} %bitcast.5) | data formatting | bytes 2359296

commit v7 on v6

--- a/solution.py
+++ b/solution.py
@@ -284,13 +284,11 @@
     def edge_left(source, part):
         return block_copy(source, 13, part, left_s.at[3, part], left_r.at[3, part], left)
 
-    def edge_far(kind, part):
-        return block_copy(
-            (12, 12, 13, 13)[kind], 16, part, edge_s.at[kind, part], edge_r.at[kind % 2, part],
-            (right, right, left, left)[kind], (keys_of, values_of)[kind % 2],
-        )
-
-    far_when = (x < 3, x == 2, x == 1, x > 0)
+    def far_up(part):
+        return block_copy(15, 16, part, edge_s.at[part], edge_r.at[part], up)
+
+    def far_down(part):
+        return block_copy(9, 16, part, edge_s.at[part], edge_r.at[part], down)
 
     def begin(part):
         climb(0, part).start()
@@ -313,20 +311,19 @@
         to_left(row, part).wait_recv()
         pass_values(row, part).start()
 
-    def passed(row):
-        for part in range(3):
-            pass_keys(row, part).wait_recv()
-            pass_values(row, part).wait_recv()
+    def passed(row, part):
+        pass_keys(row, part).wait_recv()
+        pass_values(row, part).wait_recv()
+        if row == 0:
+            pl.when(x > 1)(far_down(part).start)
+        elif row == 2:
+            pl.when(x < 2)(far_up(part).start)
 
     def got_right(part):
         edge_right(0, part).wait_recv()
-        for kind in (0, 1):
-            pl.when(far_when[kind])(edge_far(kind, part).start)
 
     def got_left(part):
         edge_left(0, part).wait_recv()
-        for kind in (2, 3):
-            pl.when(far_when[kind])(edge_far(kind, part).start)
 
     def late_edge(part):
         pl.when(x == 0)(lambda: got_right(part))
@@ -434,23 +431,25 @@
             spread(1, 2)
             late_edge(0)
         elif step == 9:
-            passed(0)
+            for part in range(3):
+                passed(0, part)
         elif step == 10:
             spread(2, 2)
             late_edge(1)
+            passed(2, 0)
         elif step == 12:
             late_edge(2)
+            passed(2, 1)
         elif step == 14:
-            passed(1)
-        elif step == 15:
-            passed(2)
+            for part in range(3):
+                passed(1, part)
+            passed(2, 2)
         elif step == 16:
             for part in range(3):
-                for kind in range(2):
-                    edge_far(kind, part).wait_recv()
+                far_up(part).wait_recv()
 
     def visit(step, carried):
-        for number in (1, 2, 3, 5, 6, 7, 9, 10, 12, 14, 15, 16):
+        for number in (1, 2, 3, 5, 6, 7, 9, 10, 12, 14, 16):
             pl.when(step == number)(functools.partial(turn, number))
         keys = meta[0, step] + key_token
         listed = meta[1, step] == 1
@@ -584,8 +583,7 @@
             pass_values(row, part).wait_send()
         edge_right(0, part).wait_send()
         edge_left(0, part).wait_send()
-        for kind in range(4):
-            pl.when(far_when[kind])(edge_far(kind, part).wait_send)
+        far_up(part).wait_send()
 
     @pl.when(section == 0)
     def _():
@@ -644,7 +642,7 @@
             dma((2, 4, 4)), dma((2, 4, 4)), dma((2, 4)), dma((2, 4)), dma((2, ZS)), dma((2, ZS)), dma((ZS,)), dma((ZS,)),
             dma((3,)), dma((3,)), dma((4,)), dma((3,)), dma((3,)),
             dma((4, 3)), dma((4, 3)), dma((4, 3)), dma((4, 3)), dma((4, 3)), dma((4, 3)),
-            dma((3, 3)), dma((3, 3)), dma((3, 3)), dma((3, 3)), dma((4, 3)), dma((2, 3)),
+            dma((3, 3)), dma((3, 3)), dma((3, 3)), dma((3, 3)), dma((3,)), dma((3,)),
         ]
         + [dma((2, PIECES))] * 6,
         compiler_params=pltpu.CompilerParams(

time: 139 us -> 141 us (1.014)
  Pallas kernels: 136 us -> 138 us
    pallas_call x1, Pallas kernels: 136 us -> 138 us  [layer(): pl.pallas_call(layer_kernel, out_shape=jax.ShapeDtypeStruct((rows, width)...]
where the time goes in v7:
time: 141 us
  Pallas kernels  138 us (98%)
  local copies, waits for them, and re-layouts  2.36 us (2%)
    pallas_call x1, Pallas kernels, layer(): pl.pallas_call(layer_kernel, out_shape=jax.ShapeDtypeStruct((rows, width)...  138 us

profile of v7, /device:TPU:1, one launch (start us, length us, event | category | flops | bytes accessed | tf_op | source)
XLA Modules:
  0.0 140.7 jit_solution(4357026848065365845)
XLA Ops:
  0.0 138.3 %layer.1 = bf16[128,4608]{1,0:T(8,128)(2,1)} custom-call(s32[32,32]{1,0:T(8,128)} %table.1, bf16[128,4608]{1,0:T(8,128)(2,1)} %bitcast.8, f32[1,4608]{1,0:T(1,128)} %gain_ref.1, s32[128,128]{1,0:T(8,128)} %bitcast.9, f32[1,128]{1,0:T(1,128)} %constant.9.frequency_ref, bf16[4608,512]{1,0:T(8,128)(2,1)} %bitcast.6, bf16[144,2,256]{2,1,0:T(2,128)(2,1)} %share_ref.1, ...), custom_call_target="tpu_custom_call" | custom-call | tf_op jit(solution)/shard_map/layer/pallas_call | solution.py:617
  138.4 2.4 %copy.11 = bf16[1,128,4608]{2,1,0:T(8,128)(2,1)} copy(bf16[1,128,4608]{2,1,0:T(8,128)(2,1)} %bitcast.5) | data formatting | bytes 2359296

commit v8 on v6

--- a/solution.py
+++ b/solution.py
@@ -377,14 +377,14 @@
     spread(0, 0)
     climbed(1, 0)
     fetch_out.start()
-    pl.when(section == 0)(lambda: make_queries(1, 2))
+    for part in range(PIECES):
+        for side in range(2):
+            row_copy(side, 2, part).wait_recv()
+    give_keys(2, 3, 1)
     climbed(2, 0)
     climbed(0, 1)
     spread(1, 0)
-    for part in range(PIECES):
-        for side in range(2):
-            row_copy(side, 2, part).wait_recv()
-    give_keys(2, 3, 1)
+    pl.when(section == 0)(lambda: make_queries(1, 2))
     spread(0, 1)
     climbed(1, 1)
     make_queries(3, 1)

time: 139 us -> 144 us (1.036)
  Pallas kernels: 136 us -> 142 us
    pallas_call x1, Pallas kernels: 136 us -> 142 us  [layer(): pl.pallas_call(layer_kernel, out_shape=jax.ShapeDtypeStruct((rows, width)...]
where the time goes in v8:
time: 144 us
  Pallas kernels  142 us (99%)
  local copies, waits for them, and re-layouts  2.36 us (2%)
    pallas_call x1, Pallas kernels, layer(): pl.pallas_call(layer_kernel, out_shape=jax.ShapeDtypeStruct((rows, width)...  142 us

profile of v8, /device:TPU:1, one launch (start us, length us, event | category | flops | bytes accessed | tf_op | source)
XLA Modules:
  0.0 144.3 jit_solution(3217893887908513593)
XLA Ops:
  0.0 142.0 %layer.1 = bf16[128,4608]{1,0:T(8,128)(2,1)} custom-call(s32[32,32]{1,0:T(8,128)} %table.1, bf16[128,4608]{1,0:T(8,128)(2,1)} %bitcast.8, f32[1,4608]{1,0:T(1,128)} %gain_ref.1, s32[128,128]{1,0:T(8,128)} %bitcast.9, f32[1,128]{1,0:T(1,128)} %constant.9.frequency_ref, bf16[4608,512]{1,0:T(8,128)(2,1)} %bitcast.6, bf16[144,2,256]{2,1,0:T(2,128)(2,1)} %share_ref.1, ...), custom_call_target="tpu_custom_call" | custom-call | tf_op jit(solution)/shard_map/layer/pallas_call | solution.py:619
  142.0 2.4 %copy.11 = bf16[1,128,4608]{2,1,0:T(8,128)(2,1)} copy(bf16[1,128,4608]{2,1,0:T(8,128)(2,1)} %bitcast.5) | data formatting | bytes 2359296
